TPU v7x, 128 devices: a whole 4x4x4 slice. The times are simulated.
128 devices in a mesh: fsdp: 4 (over x_hi, core), ctx: 32 (over y, z, x_lo).
Axes of the slice: x: 4 (x_hi: 2, x_lo: 2; x = x_hi * 2 + x_lo), y: 4, z: 4, core: 2. Of those that a mesh axis runs over, the one named last changes fastest.
Arguments:
- query_branch: bfloat16 [4, 8192, 4096], P('fsdp', 'ctx'), may hold values from -6 to 6
- key_branch: bfloat16 [4, 8192, 4096], P('fsdp', 'ctx'), may hold values from -6 to 6
- value_branch: bfloat16 [4, 8192, 4096], P('fsdp', 'ctx'), may hold values from -6 to 6
- cotangent: bfloat16 [4, 8192, 4096], P('fsdp', 'ctx'), may hold values from -6 to 6
- quantized_weight_codes: int32 [4096, 4096], P('ctx', 'fsdp'), may hold values from 0 to 15
- scale_code_bytes: int32 [4096, 64], P('ctx', 'fsdp'), may hold values from 0 to 255
- row_scale_second: float32 [4096], P('ctx'), may hold values from 0.01 to 0.1
- filters: bfloat16 [256, 128], replicated, may hold values from -0.5 to 0.5
- channel_skip_weight: float32 [4096], replicated, may hold values from -6 to 6
- adapter_down_weight: bfloat16 [4096, 64], P('ctx'), may hold values from -0.09375 to 0.09375
- adapter_up_weight: bfloat16 [64, 4096], P(None, 'fsdp'), may hold values from -0.75 to 0.75
Outputs:
- output: bfloat16 [4, 8192, 4096], P('fsdp', 'ctx')
- grad_query: bfloat16 [4, 8192, 4096], P('fsdp', 'ctx')
- grad_key: bfloat16 [4, 8192, 4096], P('fsdp', 'ctx')
- grad_value: bfloat16 [4, 8192, 4096], P('fsdp', 'ctx')
- grad_down: bfloat16 [4096, 64], P('ctx')
- grad_up: bfloat16 [64, 4096], P(None, 'fsdp')
All inputs are finite; a program needn't handle non-finite values.
Results may differ from a plain program's by a relative error of at most 0.0067.
Values may be sent and summed in bfloat16 or wider, within the bound.
No kernel may reach another device: no remote copies, remote signals or barrier semaphores. Data moves between devices by JAX's collectives and lax.ppermute only.
A program may use at most 256 MiB of HBM per device.

v0:
```python
import math

import jax
import jax.numpy as jnp
from jax import lax
from jax.sharding import PartitionSpec as P

QBLOCK = 64


normal_levels = (
    -1.0,
    -0.6961928009986877,
    -0.5250730514526367,
    -0.39491748809814453,
    -0.28444138169288635,
    -0.18477343022823334,
    -0.09105003625154495,
    0.0,
    0.07958029955625534,
    0.16093020141124725,
    0.24611230194568634,
    0.33791524171829224,
    0.44070982933044434,
    0.5626170039176941,
    0.7229568362236023,
    1.0,
)
adapter_scale = 0.25


def from_behind(shard, axis, by):
    count = lax.axis_size(axis)
    pairs = [(i, i + by) for i in range(count) if 0 <= i + by < count]
    return lax.ppermute(shard, axis, pairs)


def dequantize(quantized_weight_codes, scale_code_bytes, row_scale_second):
    levels = jnp.zeros(quantized_weight_codes.shape, jnp.float32)
    for number in range(16):
        levels = jnp.where(quantized_weight_codes == number, normal_levels[number], levels)
    absmax = row_scale_second[:, None] * (scale_code_bytes.astype(jnp.float32) + 1.0) / 256.0
    absmax = jnp.repeat(absmax, QBLOCK, axis=1)
    return (levels * absmax).astype(jnp.bfloat16)


def toeplitz(filter_taps, filter_len):
    groups = filter_taps.shape[0]
    padded = jnp.concatenate([filter_taps, jnp.zeros((groups, filter_len), filter_taps.dtype)], 1)
    repeated = jnp.tile(padded, (1, filter_len))[:, : filter_len * (2 * filter_len - 1)]
    return repeated.reshape(groups, filter_len, 2 * filter_len - 1)


def block_conv(extended, toep, filter_len):
    row_count = extended.shape[0] - (filter_len - 1)
    blocks = row_count // filter_len
    current = extended[:row_count].reshape(blocks, filter_len, -1)
    following = jnp.concatenate(
        [extended[filter_len:], jnp.zeros((1, extended.shape[1]), extended.dtype)], 0
    )
    following = following.reshape(blocks, filter_len, -1)[:, : filter_len - 1]
    windows = jnp.concatenate([current, following], 1)
    windows = windows.reshape(blocks, 2 * filter_len - 1, toep.shape[0], -1)
    result = jnp.einsum("gts,bsgk->btgk", toep, windows, preferred_element_type=jnp.float32)
    return result.reshape(row_count, -1)


def local(
    query_branch,
    key_branch,
    value_branch,
    cotangent,
    quantized_weight_codes,
    scale_code_bytes,
    row_scale_second,
    filters,
    channel_skip_weight,
    adapter_down_weight,
    adapter_up_weight,
):
    filter_len = filters.shape[1]
    queries = query_branch[0]
    output_gradient = cotangent[0]
    row_count, channels = queries.shape
    token_count = query_branch.shape[0] * row_count * lax.axis_size("ctx") * lax.axis_size("fsdp")
    multiplier = adapter_scale / math.sqrt(token_count)
    query_float = queries.astype(jnp.float32)
    key_float = key_branch[0].astype(jnp.float32)
    value_float = value_branch[0].astype(jnp.float32)
    mixed = (key_float * value_float).astype(jnp.bfloat16)
    before = from_behind(mixed[row_count - (filter_len - 1) :], "ctx", 1)
    ahead_toep = toeplitz(jnp.flip(filters, 1), filter_len)
    back_toep = toeplitz(filters, filter_len)
    gated = block_conv(
        jnp.concatenate([before, mixed], 0), ahead_toep, filter_len
    ) + channel_skip_weight * mixed.astype(jnp.float32)
    gated_signal = (query_float * gated).astype(jnp.bfloat16)
    local_piece = dequantize(quantized_weight_codes, scale_code_bytes, row_scale_second)
    local_rows, up_complete = (
        lax.all_gather(local_piece, "fsdp", axis=1, tiled=True),
        lax.all_gather(adapter_up_weight, "fsdp", axis=1, tiled=True),
    )
    backward_up_term = jnp.einsum(
        "td,rd->tr", output_gradient, up_complete, preferred_element_type=jnp.float32
    ).astype(jnp.bfloat16)
    weight_rows = lax.all_gather(local_rows, "ctx", axis=0, tiled=True)
    rank_rows = lax.all_gather(adapter_down_weight, "ctx", axis=0, tiled=True)
    output_total = jnp.dot(gated_signal, weight_rows, preferred_element_type=jnp.float32)
    down_sum = jnp.dot(gated_signal, rank_rows, preferred_element_type=jnp.float32)
    elementwise_product = jnp.einsum(
        "td,cd->tc", output_gradient, weight_rows, preferred_element_type=jnp.float32
    )
    elementwise_product = elementwise_product + adapter_scale * jnp.einsum(
        "tr,cr->tc", backward_up_term, rank_rows, preferred_element_type=jnp.float32
    )
    down_projection = down_sum.astype(jnp.bfloat16)
    output = (
        output_total
        + adapter_scale * jnp.dot(down_projection, up_complete, preferred_element_type=jnp.float32)
    ).astype(jnp.bfloat16)
    grad_query = (elementwise_product * gated).astype(jnp.bfloat16)
    grad_gated = (elementwise_product * query_float).astype(jnp.bfloat16)
    leading = jnp.concatenate(
        [jnp.zeros((filter_len, channels), jnp.bfloat16), grad_gated[: filter_len - 1]], 0
    )
    spill = block_conv(leading, back_toep, filter_len)
    arrived = from_behind(spill[1:], "ctx", -1)
    tail_rows = jnp.concatenate(
        [grad_gated, jnp.zeros((filter_len - 1, channels), jnp.bfloat16)], 0
    )
    local_grad = block_conv(tail_rows, back_toep, filter_len)
    local_grad = local_grad + jnp.concatenate(
        [jnp.zeros((row_count - filter_len + 1, channels), jnp.float32), arrived], 0
    )
    grad_mixed = local_grad + channel_skip_weight * grad_gated.astype(jnp.float32)
    grad_key = (grad_mixed * value_float).astype(jnp.bfloat16)
    grad_value = (grad_mixed * key_float).astype(jnp.bfloat16)
    term_down = multiplier * jnp.einsum(
        "tc,tr->cr", gated_signal, backward_up_term, preferred_element_type=jnp.float32
    )
    term_up = multiplier * jnp.einsum(
        "tr,td->rd", down_projection, output_gradient, preferred_element_type=jnp.float32
    )
    total_down = lax.psum(term_down, "fsdp")
    grad_down = lax.psum_scatter(total_down, "ctx", scatter_dimension=0, tiled=True)
    total_up = lax.psum(term_up, "ctx")
    grad_up = lax.psum_scatter(total_up, "fsdp", scatter_dimension=1, tiled=True)
    return (
        output[None],
        grad_query[None],
        grad_key[None],
        grad_value[None],
        grad_down.astype(jnp.bfloat16),
        grad_up.astype(jnp.bfloat16),
    )


def solution(mesh):
    return jax.shard_map(
        local,
        mesh=mesh,
        in_specs=(
            P("fsdp", "ctx", None),
            P("fsdp", "ctx", None),
            P("fsdp", "ctx", None),
            P("fsdp", "ctx", None),
            P("ctx", "fsdp"),
            P("ctx", "fsdp"),
            P("ctx"),
            P(),
            P(),
            P("ctx", None),
            P(None, "fsdp"),
        ),
        out_specs=(
            P("fsdp", "ctx", None),
            P("fsdp", "ctx", None),
            P("fsdp", "ctx", None),
            P("fsdp", "ctx", None),
            P("ctx", None),
            P(None, "fsdp"),
        ),
        check_vma=False,
    )
```

profile of v0, /device:TPU:1, one launch (start us, length us, event | category | flops | bytes accessed | tf_op | source)
XLA Modules:
  0.0 1086.2 jit_solution(9586040226539737358)
XLA Ops:
  10.7 24.5 %all-gather.3.cloned.1.call-done = bf16[128,4096]{0,1:T(8,128)(2,1)} async-done(((bf16[128,1024]{0,1:T(8,128)(2,1)}), bf16[128,4096]{0,1:T(8,128)(2,1)}) %all-gather.3.cloned.1.call-update) | async-done | bytes 1048592 | tf_op jit(solution)/shard_map/all_gather | solution.py:100
  35.2 3.0 fusion.11
  38.3 1.5 slice.49
  39.8 3.2 collective-permute-start
  42.9 1.8 slice.50
  46.3 41.7 %copy.62 = bf16[32,8,128,256]{3,1,2,0:T(8,128)(2,1)S(1)} copy(bf16[32,8,128,256]{3,2,1,0:T(8,128)(2,1)S(1)} %bitcast.101) | data formatting | bytes 33554432
  88.0 6.6 slice.54
  94.6 56.8 %reshape.84 = bf16[256,128,255,1]{2,1,0,3:T(8,128)(2,1)} reshape(bf16[256,32640]{1,0:T(8,128)(2,1)} %slice.54) | data formatting | bytes 33423360 | tf_op jit(solution)/shard_map/reshape | solution.py:51
  151.3 56.7 %reshape.76 = bf16[256,128,255]{2,1,0:T(8,128)(2,1)} reshape(bf16[256,32640]{1,0:T(8,128)(2,1)} %slice.54) | data formatting | bytes 33423360 | tf_op jit(solution)/shard_map/reshape | solution.py:51
  209.3 41.7 %copy.60 = bf16[32,8,128,256]{3,1,2,0:T(8,128)(2,1)S(1)} copy(bf16[32,8,128,256]{3,2,1,0:T(8,128)(2,1)S(1)} %bitcast.102) | data formatting | bytes 33554432
  251.0 6.6 slice.52
  257.6 56.8 %reshape.83 = bf16[256,128,255,1]{2,1,0,3:T(8,128)(2,1)} reshape(bf16[256,32640]{1,0:T(8,128)(2,1)} %slice.52) | data formatting | bytes 33423360 | tf_op jit(solution)/shard_map/reshape | solution.py:51
  314.4 3.2 concatenate.45
  317.6 4.2 copy.57
  321.8 12.4 %all_gather.15 = bf16[64,4096]{1,0:T(8,128)(2,1)S(1)} all-gather(bf16[64,1024]{1,0:T(8,128)(2,1)S(1)} %copy-done.11), channel_id=1, replica_groups=mesh['fsdp'=4,'ctx'=32] {'fsdp'}, dimensions={1}, use_global_device_ids=true | all-gather | bytes 655360 | tf_op jit(solution)/shard_map/all_gather | solution.py:101
  334.1 80.4 %all_gather.14 = bf16[4096,64]{0,1:T(8,128)(2,1)S(1)} all-gather(bf16[128,64]{0,1:T(8,128)(2,1)S(1)} %copy-done.13), channel_id=1, replica_groups=mesh['fsdp'=4,'ctx'=32] {'ctx'}, dimensions={0}, use_global_device_ids=true | all-gather | bytes 540672 | tf_op jit(solution)/shard_map/all_gather | solution.py:107
  415.3 2.9 pad_maximum_fusion
  418.2 4.1 copy.23
  422.3 4.0 concatenate.44
  426.3 3.4 copy.25
  429.7 9.5 fusion.19
  439.2 2.2 copy.27
  441.3 2.2 copy.73
  443.6 5.7 copy.28
  449.2 329.5 %all-gather.5.cloned.1.call-done = bf16[4096,4096]{0,1:T(8,128)(2,1)} async-done(((bf16[128,4096]{0,1:T(8,128)(2,1)}), bf16[4096,4096]{0,1:T(8,128)(2,1)}) %all-gather.5.cloned.1.call-update) | async-done | bytes 33554448 | tf_op jit(solution)/shard_map/all_gather | solution.py:106
  778.8 17.2 %convolution_bitcast_fusion = f32[256,4096]{1,0:T(8,128)} fusion(bf16[4096,4096]{0,1:T(8,128)(2,1)} %all-gather.5.cloned.1.call-done, bf16[1,256,4096]{2,1,0:T(8,128)(2,1)S(1)} %copy-done), kind=kOutput, calls=%fused_computation.4 | convolution fusion | flops 8589934592 | bytes 39845888 | tf_op jit(solution)/shard_map/td,cd->tc/dot_general | solution.py:110
  796.0 6.7 fusion.29
  806.5 2.3 fusion.39
  808.9 2.3 copy.59
  811.2 2.8 concatenate.56.clone
  814.0 12.6 %convolution_bitcast_fusion.1 = f32[1,128,256,16]{1,3,2,0:T(8,128)} fusion(bf16[255,256,16]{0,2,1:T(8,128)(2,1)} %bitcast.111, bf16[256,128,255]{2,1,0:T(8,128)(2,1)} %reshape.76), kind=kOutput, calls=%fused_computation.45 | convolution fusion | flops 267386880 | bytes 20897792 | tf_op jit(solution)/shard_map/gts,bsgk->btgk/dot_general | solution.py:64
  826.6 3.7 slice.57
  830.3 3.0 copy.52
  834.5 3.1 convolution_multiply_fusion.2
  837.6 17.7 %fusion.43 = f32[256,4096]{1,0:T(8,128)} fusion(bf16[256,4096]{1,0:T(8,128)(2,1)} %copy-done.6, bf16[4096,4096]{0,1:T(8,128)(2,1)} %all-gather.5.cloned.1.call-done), kind=kOutput, calls=%fused_computation.55 | convolution fusion | flops 8589934592 | bytes 39845888 | tf_op jit(solution)/shard_map/dot_general | solution.py:108
  855.3 4.1 copy.46
  859.4 4.0 concatenate.49
  863.3 3.3 copy.48
  866.9 1.5 concatenate.51
  868.3 4.2 copy.58
  872.5 9.9 fusion.24
  882.4 2.2 copy.50
  884.6 2.3 copy.72
  886.9 5.7 copy.53
  892.5 4.4 fusion.7
  896.9 6.5 fusion.30
  903.4 135.5 %all-reduce.8 = bf16[64,1024]{1,0:T(8,128)(2,1)} all-reduce(f32[64,1024]{1,0:T(8,128)} %reduce-scatter.5.cloned.1.call-done), channel_id=1, replica_groups=mesh['fsdp'=4,'ctx'=32] {'ctx'}, use_global_device_ids=true, to_apply=%region_2.3 | all-reduce | flops 65536 | bytes 393216 | tf_op jit(solution)/shard_map/psum | solution.py:146
  1038.9 40.4 %psum.16 = bf16[128,64]{0,1:T(8,128)(2,1)} all-reduce(f32[128,64]{0,1:T(8,128)} %reduce-scatter.3.cloned.1.call-done), channel_id=1, replica_groups=mesh['fsdp'=4,'ctx'=32] {'fsdp'}, use_global_device_ids=true, to_apply=%region_0.1 | all-reduce | flops 8192 | bytes 49152 | tf_op jit(solution)/shard_map/psum | solution.py:144
  (55 shorter events, 12.4 us)
Async XLA Ops:
  7.2 407.4 %copy-start = (bf16[1,256,4096]{2,1,0:T(8,128)(2,1)S(1)}, bf16[1,256,4096]{2,1,0:T(8,128)(2,1)}, u32[]{:S(2)}) copy-start(bf16[1,256,4096]{2,1,0:T(8,128)(2,1)} %param.14) | copy-start | bytes 6291460
  7.2 28.0 %all-gather.3.cloned.1.call-start = ((), (), s32[]{:S(2)}) async-start(), calls=%async_computation.2 | async-start | bytes 1310720 | tf_op jit(solution)/shard_map/all_gather | solution.py:100
  10.6 768.1 %all-gather.5.cloned.1.call-start = ((), (), s32[]{:S(2)}) async-start(), calls=%async_computation.3 | async-start | bytes 34603008 | tf_op jit(solution)/shard_map/all_gather | solution.py:106
  35.2 868.2 %reduce-scatter.5.cloned.1.call-start = ((), (), s32[]{:S(2)}) async-start(), calls=%async_computation.5 | async-start | bytes 1310720 | tf_op jit(solution)/shard_map/reduce_scatter | solution.py:147
  38.2 4.7 copy-start.3
  38.2 6.5 copy-start.10
  39.8 375.6 %collective-permute-start = (bf16[127,4096]{1,0:T(8,128)(2,1)}, bf16[127,4096]{1,0:T(8,128)(2,1)}, u32[]{:S(2)}, u32[]{:S(2)}) collective-permute-start(bf16[127,4096]{1,0:T(8,128)(2,1)} %slice.49), channel_id=1, source_target_pairs={{0,1},{1,2},{2,3},{3,4},{4,5},{5,6},{6,7},{7,8},{8,9},{9,10},{10,1... | collective-permute-start | bytes 3121160 | tf_op jit(solution)/shard_map/ppermute | solution.py:35
  314.4 7.4 copy-start.11
  314.4 19.7 %copy-start.13 = (bf16[128,64]{0,1:T(8,128)(2,1)S(1)}, bf16[128,64]{0,1:T(8,128)(2,1)}, u32[]{:S(2)}) copy-start(bf16[128,64]{0,1:T(8,128)(2,1)} %param.20) | copy-start | bytes 49156
  321.8 93.6 %copy-start.4 = (bf16[256,4096]{1,0:T(8,128)(2,1)S(1)}, bf16[256,4096]{1,0:T(8,128)(2,1)}, u32[]{:S(2)}) copy-start(bf16[256,4096]{1,0:T(8,128)(2,1)} %copy-done.3) | copy-start | bytes 6291460
  426.3 3.4 copy-start.7
  449.2 346.7 %copy-start.12 = (f32[4096]{0:T(1024)S(1)}, f32[4096]{0:T(1024)}, u32[]{:S(2)}) copy-start(f32[4096]{0:T(1024)} %param.19) | copy-start | bytes 49156
  778.8 17.2 %copy-start.5 = (bf16[256,4096]{1,0:T(8,128)(2,1)S(1)}, bf16[256,4096]{1,0:T(8,128)(2,1)}, u32[]{:S(2)}) copy-start(bf16[256,4096]{1,0:T(8,128)(2,1)} %copy-done.3) | copy-start | bytes 6291460
  778.8 17.2 %copy-start.9 = (f32[256,4096]{1,0:T(8,128)S(1)}, f32[256,4096]{1,0:T(8,128)}, u32[]{:S(2)}) copy-start(f32[256,4096]{1,0:T(8,128)} %copy.28) | copy-start | bytes 12582916
  802.7 1.3 copy-start.6
  802.7 3.8 copy-start.14
  806.2 232.7 %reduce-scatter.3.cloned.1.call-start = ((), (), s32[]{:S(2)}) async-start(), calls=%async_computation.4 | async-start | bytes 1081344 | tf_op jit(solution)/shard_map/reduce_scatter | solution.py:145
  833.2 63.7 %collective-permute-start.1 = (f32[127,4096]{1,0:T(8,128)}, f32[127,4096]{1,0:T(8,128)}, u32[]{:S(2)}, u32[]{:S(2)}) collective-permute-start(f32[127,4096]{1,0:T(8,128)} %copy.52), channel_id=1, source_target_pairs={{1,0},{2,1},{3,2},{4,3},{5,4},{6,5},{7,6},{8,7},{9,8},{10,9},{11,1... | collective-permute-start | bytes 6242312 | tf_op jit(solution)/shard_map/ppermute | solution.py:35
  863.3 3.3 copy-start.1
  892.5 4.4 copy-start.2
  892.5 4.4 copy-start.8
Sparse Core Ops, SparseCore 0:
  10.8 24.3 all-gather.2
  36.7 742.0 all-gather.4
  806.4 30.7 reduce-scatter.4
  839.4 139.4 reduce-scatter.2
where the time goes:
time: 1100 us; the launch traced here: 1090 us
  waiting for transfers between devices  354 us (32%)
  local copies, waits for them, and re-layouts  344 us (31%)
  blocking collectives  269 us (24%)
  matrix products  84 us (8%)
  other arithmetic  16.8 us (2%)
  between operations  14.3 us (1%)
    all_gather x1, waiting for transfers between devices, local(): weight_rows = lax.all_gather(local_rows, 'ctx', axis=0, tiled=True)  330 us
    reshape x3, local copies, waits for them, and re-layouts, toeplitz(): return repeated.reshape(groups, filter_len, 2 * filter_len - 1)  170 us
    psum x1, blocking collectives, local(): total_up = lax.psum(term_up, 'ctx')  135 us
    unnamed x38, local copies, waits for them, and re-layouts  101 us
    all_gather x1, blocking collectives, local(): rank_rows = lax.all_gather(adapter_down_weight, 'ctx', axis=0, tiled=True)  80.4 us
    psum x1, blocking collectives, local(): total_down = lax.psum(term_down, 'fsdp')  40.4 us
    dot_general x3, matrix products, block_conv(): jnp.einsum('gts,bsgk->btgk', toep, windows, preferred_element_type=jnp.fl...  32 us
    all_gather x1, waiting for transfers between devices, local(): lax.all_gather(local_piece, 'fsdp', axis=1, tiled=True)  24.5 us
  transfers between devices with their start and end apart: 6, of which 2 were waited for; matrix products, arithmetic and copies ran while one was open for 38% of the time, Pallas kernels for 0%

commit v1 on v0

v1 whole, which is shorter than its diff:
```python
import functools
import math

import jax
import jax.numpy as jnp
from jax import lax
from jax.experimental import pallas as pl
from jax.experimental.pallas import tpu as pltpu
from jax.sharding import PartitionSpec as P

QBLOCK = 64
BOTH = ("fsdp", "ctx")
RING = (0, 3, 1, 2)

normal_levels = (
    -1.0,
    -0.6961928009986877,
    -0.5250730514526367,
    -0.39491748809814453,
    -0.28444138169288635,
    -0.18477343022823334,
    -0.09105003625154495,
    0.0,
    0.07958029955625534,
    0.16093020141124725,
    0.24611230194568634,
    0.33791524171829224,
    0.44070982933044434,
    0.5626170039176941,
    0.7229568362236023,
    1.0,
)
adapter_scale = 0.25


def device_index(x, y, z, c):
    return ((x // 2) * 2 + c) * 32 + y * 8 + z * 2 + x % 2


def ring_pairs(axis0, axis1, step):
    pairs = []
    for x in range(4):
        for y in range(4):
            for z in range(4):
                for c in range(2):
                    to = [x, y, z]
                    axis = (axis0, axis1)[c]
                    to[axis] = (to[axis] + step) % 4
                    pairs.append((device_index(x, y, z, c), device_index(*to, c)))
    return pairs


def send(block, axis0, axis1, step):
    return lax.ppermute(block, BOTH, ring_pairs(axis0, axis1, step))


def swap_cores(block):
    pairs = [
        (device_index(x, y, z, c), device_index(x, y, z, 1 - c))
        for x in range(4)
        for y in range(4)
        for z in range(4)
        for c in range(2)
    ]
    return lax.ppermute(block, BOTH, pairs)


def ring_phase(block, axis0, axis1):
    half = block.shape[0] // 2
    plus = send(block, axis0, axis1, 1)
    minus = send(block, axis0, axis1, -1)
    far_low = send(plus[:half], axis0, axis1, 1)
    far_high = send(minus[half:], axis0, axis1, -1)
    return plus, minus, far_low, far_high


def along_ctx(shard, by):
    pairs = [(i, i + by) for i in range(32) if 0 <= i + by < 32]
    return lax.ppermute(shard, "ctx", pairs)


def weight_piece(codes, scale_bytes, row_scale, down, up):
    levels = jnp.zeros(codes.shape, jnp.float32)
    for number in range(16):
        levels = jnp.where(codes == number, normal_levels[number], levels)
    absmax = row_scale[:, None] * (scale_bytes.astype(jnp.float32) + 1.0) / 256.0
    absmax = jnp.repeat(absmax, QBLOCK, axis=1)
    weight = (levels * absmax).astype(jnp.bfloat16).astype(jnp.float32)
    low_rank = jnp.dot(down, up, preferred_element_type=jnp.float32)
    return (weight + adapter_scale * low_rank).astype(jnp.bfloat16)


def toeplitz_conv(base, window, width):
    lane = lax.broadcasted_iota(jnp.int32, (128, 2 * width), 1)
    group_of = (lane % width) // 16
    total = None
    for group in range(width // 16):
        row = jnp.broadcast_to(base[group : group + 1, :], (128, 256))
        toep = pltpu.roll(row, 0, 1, stride=1, stride_axis=0).astype(jnp.bfloat16)
        part = jnp.dot(toep, window, preferred_element_type=jnp.float32)
        total = part if total is None else jnp.where(group_of == group, part, total)
    return total


def forward_kernel(base_ref, skip_ref, query_ref, key_ref, value_ref, halo_ref, gated_ref, signal_ref, *, tiles):
    for tile in range(tiles):
        lanes = pl.ds(tile * 128, 128)
        mixed = (
            key_ref[:, lanes].astype(jnp.float32) * value_ref[:, lanes].astype(jnp.float32)
        ).astype(jnp.bfloat16)
        first = jnp.concatenate([halo_ref[:, lanes], mixed[:128]], 0)
        window = jnp.concatenate([first, mixed], 1)
        conv = toeplitz_conv(base_ref[pl.ds(tile * 8, 8), :], window, 128)
        conv = jnp.concatenate([conv[:, :128], conv[:, 128:]], 0)
        gated = conv + skip_ref[:, lanes] * mixed.astype(jnp.float32)
        gated_ref[:, lanes] = gated
        signal_ref[:, lanes] = (query_ref[:, lanes].astype(jnp.float32) * gated).astype(jnp.bfloat16)


def forward_conv(base, skip, query, key, value, halo):
    rows, channels = query.shape
    width = 512
    block = pl.BlockSpec((rows, width), lambda j: (0, j))
    return pl.pallas_call(
        functools.partial(forward_kernel, tiles=width // 128),
        grid=(channels // width,),
        in_specs=[
            pl.BlockSpec((width // 16, 256), lambda j: (j, 0)),
            pl.BlockSpec((1, width), lambda j: (0, j)),
            block,
            block,
            block,
            pl.BlockSpec((128, width), lambda j: (0, j)),
        ],
        out_specs=[block, block],
        out_shape=[
            jax.ShapeDtypeStruct((rows, channels), jnp.float32),
            jax.ShapeDtypeStruct((rows, channels), jnp.bfloat16),
        ],
        compiler_params=pltpu.CompilerParams(vmem_limit_bytes=32 << 20),
        cost_estimate=pl.CostEstimate(flops=1 << 32, bytes_accessed=14 << 20, transcendentals=0),
        name="forward_conv",
    )(base, skip, query, key, value, halo)


def backward_kernel(
    base_ref, skip_ref, back_ref, gated_ref, query_ref, query_halo_ref, key_ref, value_ref,
    grad_query_ref, grad_key_ref, grad_value_ref, *, tiles,
):
    rows = query_ref.shape[0]
    for tile in range(tiles):
        lanes = pl.ds(tile * 128, 128)
        back = back_ref[pl.ds(0, rows), lanes]
        grad_query_ref[:, lanes] = (back * gated_ref[:, lanes]).astype(jnp.bfloat16)
        here = (back * query_ref[:, lanes].astype(jnp.float32)).astype(jnp.bfloat16)
        ahead = back_ref[pl.ds(rows, 128), lanes] * query_halo_ref[:, lanes].astype(jnp.float32)
        second = jnp.concatenate([here[128:], ahead.astype(jnp.bfloat16)], 0)
        window = jnp.concatenate([here, second], 1)
        conv = toeplitz_conv(base_ref[pl.ds(tile * 8, 8), :], window, 128)
        conv = jnp.concatenate([conv[:, :128], conv[:, 128:]], 0)
        mixed = conv + skip_ref[:, lanes] * here.astype(jnp.float32)
        grad_key_ref[:, lanes] = (mixed * value_ref[:, lanes].astype(jnp.float32)).astype(jnp.bfloat16)
        grad_value_ref[:, lanes] = (mixed * key_ref[:, lanes].astype(jnp.float32)).astype(jnp.bfloat16)


def backward_conv(base, skip, back, gated, query, query_halo, key, value):
    rows, channels = query.shape
    width = 512
    block = pl.BlockSpec((rows, width), lambda j: (0, j))
    result = jax.ShapeDtypeStruct((rows, channels), jnp.bfloat16)
    return pl.pallas_call(
        functools.partial(backward_kernel, tiles=width // 128),
        grid=(channels // width,),
        in_specs=[
            pl.BlockSpec((width // 16, 256), lambda j: (j, 0)),
            pl.BlockSpec((1, width), lambda j: (0, j)),
            pl.BlockSpec((rows + 128, width), lambda j: (0, j)),
            block,
            block,
            pl.BlockSpec((128, width), lambda j: (0, j)),
            block,
            block,
        ],
        out_specs=[block] * 3,
        out_shape=[result] * 3,
        compiler_params=pltpu.CompilerParams(vmem_limit_bytes=32 << 20),
        cost_estimate=pl.CostEstimate(flops=1 << 32, bytes_accessed=24 << 20, transcendentals=0),
        name="backward_conv",
    )(base, skip, back, gated, query, query_halo, key, value)


def project_kernel(*refs, groups, first, last):
    refs = list(refs)
    meta = refs.pop(0)
    signal_ref, cot_ref = refs.pop(0), refs.pop(0)
    if not first:
        out_in, back_in = refs.pop(0), refs.pop(0)
    arrays = [[refs.pop(0) for _ in range(count)] for _, _, count in groups]
    out_ref, back_ref = refs.pop(0), refs.pop(0)
    signal, cot, out_acc, back_acc, held, sems, io_sems = refs
    x0, y0, z0, core = meta[0], meta[1], meta[2], meta[3]
    loads = [
        pltpu.make_async_copy(signal_ref, signal, io_sems.at[0]),
        pltpu.make_async_copy(cot_ref, cot, io_sems.at[1]),
    ]
    if not first:
        loads.append(pltpu.make_async_copy(out_in, out_acc, io_sems.at[2]))
        loads.append(pltpu.make_async_copy(back_in, back_acc, io_sems.at[3]))
    for load in loads:
        load.start()
    copies = []
    for g, (mine, _, count) in enumerate(groups):
        chain = core if mine else 1 - core
        group = []
        for n in range(16):
            a, b = RING[n // 4], RING[n % 4]
            x = (x0 + jnp.where(chain == 0, b, a)) & 3
            w = jnp.where(chain == 0, y0 + a, z0 + b) & 3
            slot = pl.multiple_of((w * 4 + x) * 128, 128)
            each = 16 // count
            source = arrays[g][n // each].at[pl.ds((n % each) * 128, 128), :]
            group.append(
                pltpu.make_async_copy(source, held.at[g, pl.ds(slot, 128), :], sems.at[g, n])
            )
        for copy in group:
            copy.start()
        copies.append(group)
    if first:
        out_acc[...] = jnp.zeros_like(out_acc)
        back_acc[...] = jnp.zeros_like(back_acc)
    for load in loads:
        load.wait()
    for g, (mine, offset, _) in enumerate(groups):
        chain = core if mine else 1 - core
        fixed = jnp.where(chain == 0, z0 + offset, y0 + offset) & 3
        for copy in copies[g]:
            copy.wait()

        @pl.loop(0, 8)
        def _(step, g=g, chain=chain, fixed=fixed):
            w, xh = step // 2, step % 2
            rows = jnp.where(chain == 0, w * 4 + fixed, fixed * 4 + w)
            rows = pl.multiple_of(rows * 256, 256)
            cols = pl.multiple_of((xh * 2 + chain) * 1024, 1024)
            weight = held[g, pl.ds(pl.multiple_of(step * 256, 256), 256), :]
            out_acc[:, pl.ds(cols, 1024)] += jnp.dot(
                signal[:, pl.ds(rows, 256)], weight, preferred_element_type=jnp.float32
            )
            back_acc[:, pl.ds(rows, 256)] += lax.dot_general(
                cot[:, pl.ds(cols, 1024)],
                weight,
                (((1,), (1,)), ((), ())),
                preferred_element_type=jnp.float32,
            )

    if last:
        signal[...] = out_acc[...].astype(jnp.bfloat16)
        stores = [pltpu.make_async_copy(signal, out_ref, io_sems.at[0])]
    else:
        stores = [pltpu.make_async_copy(out_acc, out_ref, io_sems.at[0])]
    stores.append(pltpu.make_async_copy(back_acc, back_ref, io_sems.at[1]))
    for store in stores:
        store.start()
    for store in stores:
        store.wait()


def project(meta, signal, cot, sums, groups, last):
    rows, channels = signal.shape
    first = sums is None
    arrays = [array for group in groups for array in group[2]]
    static = tuple((mine, offset, len(held)) for mine, offset, held in groups)
    anywhere = pl.BlockSpec(memory_space=pl.ANY)
    out_type = jnp.bfloat16 if last else jnp.float32
    operands = [meta, signal, cot] + ([] if first else list(sums)) + arrays
    aliases = {} if first else ({4: 1} if last else {3: 0, 4: 1})
    flops = len(groups) * 16 * 128 * 1024 * (rows + cot.shape[0]) * 2
    return pl.pallas_call(
        functools.partial(project_kernel, groups=static, first=first, last=last),
        in_specs=[pl.BlockSpec(memory_space=pltpu.SMEM)] + [anywhere] * (len(operands) - 1),
        out_specs=[anywhere, anywhere],
        out_shape=[
            jax.ShapeDtypeStruct((rows, channels), out_type),
            jax.ShapeDtypeStruct((cot.shape[0], channels), jnp.float32),
        ],
        scratch_shapes=[
            pltpu.VMEM((rows, channels), jnp.bfloat16),
            pltpu.VMEM((cot.shape[0], channels), jnp.bfloat16),
            pltpu.VMEM((rows, channels), jnp.float32),
            pltpu.VMEM((cot.shape[0], channels), jnp.float32),
            pltpu.VMEM((len(groups), 2048, 1024), jnp.bfloat16),
            pltpu.SemaphoreType.DMA((len(groups), 16)),
            pltpu.SemaphoreType.DMA((4,)),
        ],
        input_output_aliases=aliases,
        compiler_params=pltpu.CompilerParams(vmem_limit_bytes=48 << 20),
        cost_estimate=pl.CostEstimate(
            flops=flops, bytes_accessed=len(groups) * (4 << 20) + (25 << 20), transcendentals=0
        ),
        name="project",
    )(*operands)


def adapter_gradients(signal, cot, down_piece, up_piece, multiplier):
    rank = up_piece.shape[0]
    up = lax.all_gather(up_piece, "fsdp", axis=1, tiled=True)
    spread = jnp.broadcast_to(down_piece.T[None], (32, rank, 128))
    down = lax.all_to_all(spread, "ctx", 0, 0, tiled=True)
    down = jnp.transpose(down, (1, 0, 2)).reshape(rank, 4096)
    down_projection = lax.dot_general(
        signal, down, (((1,), (1,)), ((), ())), preferred_element_type=jnp.float32
    ).astype(jnp.bfloat16)
    back_up = lax.dot_general(
        cot, up, (((1,), (1,)), ((), ())), preferred_element_type=jnp.float32
    ).astype(jnp.bfloat16)
    over_rows = (((0,), (0,)), ((), ()))
    term_down = lax.dot_general(back_up, signal, over_rows, preferred_element_type=jnp.float32)
    term_up = lax.dot_general(down_projection, cot, over_rows, preferred_element_type=jnp.float32)
    parts_down = term_down.astype(jnp.bfloat16).reshape(4, 16, 32, 128)
    parts_down = jnp.transpose(parts_down, (0, 2, 1, 3)).reshape(128, 16, 128)
    parts_up = term_up.astype(jnp.bfloat16).reshape(32, 2, 4, 1024)
    parts_up = jnp.transpose(parts_up, (2, 0, 1, 3)).reshape(128, 16, 128)
    parts = jnp.concatenate([parts_down, parts_up], 1)
    parts = lax.all_to_all(parts, BOTH, 0, 0, tiled=True)
    sums = (multiplier * jnp.sum(parts.astype(jnp.float32), 0)).astype(jnp.bfloat16)
    grad_down = lax.all_gather(sums[:16], "fsdp", axis=0, tiled=True)
    mine_up = jnp.broadcast_to(sums[None, 16:], (32, 16, 128))
    grad_up = lax.all_to_all(mine_up, "ctx", 0, 0, tiled=True).reshape(rank, 1024)
    return grad_down.T, grad_up


def local(
    query_branch,
    key_branch,
    value_branch,
    cotangent,
    quantized_weight_codes,
    scale_code_bytes,
    row_scale_second,
    filters,
    channel_skip_weight,
    adapter_down_weight,
    adapter_up_weight,
):
    query, key, value, cot = query_branch[0], key_branch[0], value_branch[0], cotangent[0]
    rows, channels = query.shape
    multiplier = adapter_scale / math.sqrt(4 * 8192)
    ctx, fsdp = lax.axis_index("ctx"), lax.axis_index("fsdp")
    core = fsdp % 2
    meta = jnp.stack([(fsdp // 2) * 2 + ctx % 2, ctx // 8, (ctx // 2) % 4, core]).astype(jnp.int32)

    piece = weight_piece(
        quantized_weight_codes, scale_code_bytes, row_scale_second, adapter_down_weight, adapter_up_weight
    )
    plus, minus, low, high = ring_phase(piece, 0, 2)
    held = jnp.concatenate([piece, plus, minus, low, high], 0)
    plus, minus, low, high = ring_phase(held, 1, 0)
    held = jnp.concatenate([held, plus, minus, low, high], 0)
    plus, minus, low, high = ring_phase(held, 2, 1)

    mixed_tail = (key[128:].astype(jnp.float32) * value[128:].astype(jnp.float32)).astype(jnp.bfloat16)
    mixed_halo = along_ctx(mixed_tail, 1)
    query_halo = along_ctx(query[:128], -1)
    cot_halo = along_ctx(cot[:128], -1)

    taps = filters.astype(jnp.float32)
    forward_base = jnp.pad(jnp.flip(taps, 1), ((0, 0), (1, 127)))
    backward_base = jnp.pad(taps, ((0, 0), (0, 128)))
    skip = channel_skip_weight[None]
    gated, signal = forward_conv(forward_base, skip, query, key, value, mixed_halo)

    grad_down, grad_up = adapter_gradients(signal, cot, adapter_down_weight, adapter_up_weight, multiplier)

    cot_rows = jnp.concatenate([cot, cot_halo], 0)
    sums = project(
        meta, signal, cot_rows, None, [(True, 0, [held]), (False, 0, [swap_cores(held)])], False
    )
    sums = project(
        meta,
        signal,
        cot_rows,
        sums,
        [
            (True, -1, [plus]),
            (False, -1, [swap_cores(plus)]),
            (True, 1, [minus]),
            (False, 1, [swap_cores(minus)]),
        ],
        False,
    )
    output, back = project(
        meta,
        signal,
        cot_rows,
        sums,
        [(True, 2, [low, high]), (False, 2, [swap_cores(low), swap_cores(high)])],
        True,
    )
    grad_query, grad_key, grad_value = backward_conv(
        backward_base, skip, back, gated, query, query_halo, key, value
    )
    return output[None], grad_query[None], grad_key[None], grad_value[None], grad_down, grad_up


def solution(mesh):
    return jax.shard_map(
        local,
        mesh=mesh,
        in_specs=(
            P("fsdp", "ctx", None),
            P("fsdp", "ctx", None),
            P("fsdp", "ctx", None),
            P("fsdp", "ctx", None),
            P("ctx", "fsdp"),
            P("ctx", "fsdp"),
            P("ctx"),
            P(),
            P(),
            P("ctx", None),
            P(None, "fsdp"),
        ),
        out_specs=(
            P("fsdp", "ctx", None),
            P("fsdp", "ctx", None),
            P("fsdp", "ctx", None),
            P("fsdp", "ctx", None),
            P("ctx", None),
            P(None, "fsdp"),
        ),
        check_vma=False,
    )
```

time: 1100 us -> 322 us (0.29)
  local copies, waits for them, and re-layouts: 344 us -> 40.8 us
  waiting for transfers between devices: 354 us -> 75.7 us
  blocking collectives: 269 us -> 20.9 us
  Pallas kernels: 0 us -> 87.3 us
  matrix products: 84 us -> 10.8 us
  starting transfers between devices: 4.82 us -> 72.3 us
  between operations: 14.3 us -> 1.09 us
    all_gather x2 -> x0, waiting for transfers between devices: 354 us -> none  [the longest x1 330 us: local(): weight_rows = lax.all_gather(local_rows, 'ctx', axis=0, tiled=True)]
    psum x2 -> x0, blocking collectives: 176 us -> none  [the longest x1 135 us: local(): total_up = lax.psum(term_up, 'ctx')]
    reshape x5 -> x6, local copies, waits for them, and re-layouts: 182 us -> 7.76 us  [the longest x2 4.46 us: adapter_gradients(): parts_up = term_up.astype(jnp.bfloat16).reshape(32, 2, 4, 1024)]
    pallas_call x0 -> x5, Pallas kernels: none -> 87.3 us  [the longest x3 66.4 us: project(): pl.pallas_call(functools.partial(project_kernel, groups=static, first=fir...]
    unnamed x38 -> x46, local copies, waits for them, and re-layouts: 101 us -> 18.5 us
    dot_general x11 -> x3, matrix products: 84 us -> 10.8 us  [the longest x1 4.2 us: adapter_gradients(): lax.dot_general(down_projection, cot, over_rows, preferred_element_type=j...]
    all_gather x2, blocking collectives: 92.8 us -> 20.9 us  [the longest x1 14 us: adapter_gradients(): up = lax.all_gather(up_piece, 'fsdp', axis=1, tiled=True)]
    ppermute x2 -> x20, waiting for transfers between devices: 0.01 us -> 58.7 us  [the longest x12 58.7 us: send(): return lax.ppermute(block, BOTH, ring_pairs(axis0, axis1, step))]
  transfers between devices with their start and end apart: 6 -> 23, of which waited for: 2 -> 6; matrix products, arithmetic and copies ran while one was open for 38% -> 13% of each run, Pallas kernels for 0% -> 24%
where the time goes in v1:
time: 322 us; the launch traced here: 317 us
  Pallas kernels  87.3 us (27%)
  waiting for transfers between devices  75.7 us (24%)
  starting transfers between devices  72.3 us (22%)
  local copies, waits for them, and re-layouts  40.8 us (13%)
  blocking collectives  20.9 us (6%)
  matrix products  10.8 us (3%)
  other arithmetic  8.23 us (3%)
    pallas_call x3, Pallas kernels, project(): pl.pallas_call(functools.partial(project_kernel, groups=static, first=fir...  66.4 us
    ppermute x12, waiting for transfers between devices, send(): return lax.ppermute(block, BOTH, ring_pairs(axis0, axis1, step))  58.7 us
    ppermute x5, starting transfers between devices, swap_cores(): return lax.ppermute(block, BOTH, pairs)  30.7 us
    unnamed x46, local copies, waits for them, and re-layouts  18.5 us
    ppermute x12, starting transfers between devices, send(): return lax.ppermute(block, BOTH, ring_pairs(axis0, axis1, step))  18.3 us
    all_to_all x1, waiting for transfers between devices, adapter_gradients(): parts = lax.all_to_all(parts, BOTH, 0, 0, tiled=True)  17 us
    all_gather x1, blocking collectives, adapter_gradients(): up = lax.all_gather(up_piece, 'fsdp', axis=1, tiled=True)  14 us
    pallas_call x1, Pallas kernels, backward_conv(): pl.pallas_call(functools.partial(backward_kernel, tiles=width // 128), gr...  11.5 us
  transfers between devices with their start and end apart: 23, of which 6 were waited for; matrix products, arithmetic and copies ran while one was open for 13% of the time, Pallas kernels for 24%

profile of v1, /device:TPU:1, one launch (start us, length us, event | category | flops | bytes accessed | tf_op | source)
XLA Modules:
  0.0 317.2 jit_solution(4315754154088647908)
XLA Ops:
  1.6 2.6 constant_dynamic-update-slice_fusion.4
  4.1 2.5 collective-permute-start.2
  6.6 2.1 collective-permute-start.3
  8.7 4.0 %collective-permute-done.2 = bf16[128,1024]{1,0:T(8,128)(2,1)S(1)} collective-permute-done((bf16[128,1024]{1,0:T(8,128)(2,1)S(1)}, bf16[128,1024]{1,0:T(8,128)(2,1)S(1)}, u32[]{:S(2)}, u32[]{:S(2)}) %collective-permute-start.2) | collective-permute-done | bytes 262176 | tf_op jit(solution)/shard_map/ppermute | solution.py:54
  12.9 2.7 collective-permute-start.5
  20.2 2.0 collective-permute-start.7
  22.2 12.5 %collective-permute-done.6 = bf16[512,1024]{1,0:T(8,128)(2,1)S(1)} collective-permute-done((bf16[512,1024]{1,0:T(8,128)(2,1)S(1)}, bf16[512,1024]{1,0:T(8,128)(2,1)S(1)}, u32[]{:S(2)}, u32[]{:S(2)}) %collective-permute-start.6) | collective-permute-done | bytes 1048608 | tf_op jit(solution)/shard_map/ppermute | solution.py:54
  34.8 2.7 collective-permute-start.9
  39.6 4.7 %collective-permute-done.8 = bf16[256,1024]{1,0:T(8,128)(2,1)S(1)} collective-permute-done((bf16[256,1024]{1,0:T(8,128)(2,1)S(1)}, bf16[256,1024]{1,0:T(8,128)(2,1)S(1)}, u32[]{:S(2)}, u32[]{:S(2)}) %collective-permute-start.8) | collective-permute-done | bytes 524320 | tf_op jit(solution)/shard_map/ppermute | solution.py:54
  46.7 2.0 collective-permute-start.13
  48.8 1.2 fusion.3
  50.0 1.5 collective-permute-start
  51.5 5.0 %collective-permute-start.10 = (bf16[2048,1024]{1,0:T(8,128)(2,1)}, bf16[2048,1024]{1,0:T(8,128)(2,1)}, u32[]{:S(2)}, u32[]{:S(2)}) collective-permute-start(bf16[2048,1024]{1,0:T(8,128)(2,1)} %constant_dynamic-update-slice_fusion.5.refs_3_), channel_id=1, source_target_pairs={{0,32},{32,0},{2,34},{34,2},{4,36},{36,4},{6,38},{38,6},{8,40},{40... | collective-permute-start | bytes 12582920 | tf_op jit(solution)/shard_map/ppermute | solution.py:65
  57.5 1.3 collective-permute-start.1
  58.8 36.5 %collective-permute-done.11.refs_5_ = bf16[2048,1024]{1,0:T(8,128)(2,1)} collective-permute-done((bf16[2048,1024]{1,0:T(8,128)(2,1)}, bf16[2048,1024]{1,0:T(8,128)(2,1)}, u32[]{:S(2)}, u32[]{:S(2)}) %collective-permute-start.11) | collective-permute-done | bytes 4194336 | tf_op jit(solution)/shard_map/ppermute | solution.py:54
  95.3 24.5 %collective-permute-start.12 = (bf16[2048,1024]{1,0:T(8,128)(2,1)}, bf16[2048,1024]{1,0:T(8,128)(2,1)}, u32[]{:S(2)}, u32[]{:S(2)}) collective-permute-start(bf16[2048,1024]{1,0:T(8,128)(2,1)} %collective-permute-done.11.refs_5_), channel_id=1, source_target_pairs={{0,32},{32,0},{2,34},{34,2},{4,36},{36,4},{6,38},{38,6},{8,40},{40... | collective-permute-start | bytes 12582920 | tf_op jit(solution)/shard_map/ppermute | solution.py:65
  120.7 8.9 %all-to-all-start = ((bf16[32,64,128]{2,1,0:T(8,128)(2,1)}), bf16[32,64,128]{2,1,0:T(8,128)(2,1)}, u32[]{:S(2)}, u32[]{:S(2)}) async-start(bf16[32,64,128]{2,1,0:T(8,128)(2,1)} %broadcast_in_dim.103), calls=%async_computation | async-start | bytes 1048576 | tf_op jit(solution)/shard_map/all_to_all | solution.py:308
  130.1 14.0 %all_gather.6 = bf16[64,4096]{1,0:T(8,128)(2,1)S(1)} all-gather(bf16[64,1024]{1,0:T(8,128)(2,1)S(1)} %copy-done.17), channel_id=1, replica_groups=mesh['fsdp'=4,'ctx'=32] {'fsdp'}, dimensions={1}, use_global_device_ids=true | all-gather | bytes 655360 | tf_op jit(solution)/shard_map/all_gather | solution.py:306
  145.1 1.6 copy-done.3
  146.6 1.6 copy-done.6
  148.2 1.6 copy-done.8
  149.8 1.2 copy-done.14
  151.1 9.4 %forward_conv.1 = (f32[256,4096]{1,0:T(8,128)S(1)}, bf16[256,4096]{1,0:T(8,128)(2,1)S(1)}) custom-call(f32[256,256]{1,0:T(8,128)S(1)} %pad.8.base_ref, f32[1,4096]{1,0:T(1,128)S(1)} %bitcast.58, bf16[256,4096]{1,0:T(8,128)(2,1)S(1)} %bitcast.56, bf16[256,4096]{1,0:T(8,128)(2,1)S(1)} %bitcast.52, bf16[256,4096]{1,0:T(8,128)(2,1)S(1)} %bitcast.54, ...), custom_call_target="tpu_custom_call" | custom-call | flops 4294967296 | bytes 14680064 | tf_op jit(solution)/shard_map/forward_conv/pallas_call | solution.py:124
  160.4 4.6 %slice.62 = bf16[1024,1024]{1,0:T(8,128)(2,1)} slice(bf16[2048,1024]{1,0:T(8,128)(2,1)} %collective-permute-done.11.refs_5_), slice={[0:1024], [0:1024]} | slice | bytes 4194304 | tf_op jit(solution)/shard_map/slice | solution.py:72
  165.0 1.4 collective-permute-start.15
  166.4 3.1 slice.63
  169.5 1.3 collective-permute-start.16
  170.8 4.2 %convolution_convert_fusion = bf16[64,4096]{1,0:T(8,128)(2,1)} fusion(bf16[256,4096]{1,0:T(8,128)(2,1)S(1)} %get-tuple-element.17.refs_1_, bf16[1,256,4096]{2,1,0:T(8,128)(2,1)} %param.14, bf16[32,64,128]{2,1,0:T(8,128)(2,1)} %all-to-all-done), kind=kOutput, calls=%fused_computation | convolution fusion | flops 268713984 | bytes 5242880 | tf_op jit(solution)/shard_map/dot_general | solution.py:318
  175.0 2.2 reshape.48
  177.2 2.2 copy.36
  179.5 2.2 reshape.49
  181.7 4.0 %fusion = bf16[8,8,32,128]{3,1,2,0:T(8,128)(2,1)} fusion(bf16[256,4096]{1,0:T(8,128)(2,1)S(1)} %get-tuple-element.17.refs_1_, bf16[64,4096]{1,0:T(8,128)(2,1)S(1)} %all_gather.6, bf16[1,256,4096]{2,1,0:T(8,128)(2,1)} %param.14), kind=kOutput, calls=%fused_computation.5 | convolution fusion | flops 268713984 | bytes 5242880 | tf_op jit(solution)/shard_map/dot_general | solution.py:317
  185.7 1.1 copy.29
  187.0 2.1 pad_maximum_fusion.1
  189.1 6.3 %all-to-all-start.1 = ((bf16[128,32,128]{2,1,0:T(8,128)(2,1)}), bf16[128,32,128]{2,1,0:T(8,128)(2,1)S(1)}, u32[]{:S(2)}, u32[]{:S(2)}) async-start(bf16[128,32,128]{2,1,0:T(8,128)(2,1)} %pad_maximum_fusion.1), calls=%async_computation.1 | async-start | bytes 2097152 | tf_op jit(solution)/shard_map/all_to_all | solution.py:324
  195.5 2.3 slice_bitcast_fusion
  197.8 17.0 %all-to-all-done.1 = bf16[128,32,128]{2,1,0:T(8,128)(2,1)S(1)} async-done(((bf16[128,32,128]{2,1,0:T(8,128)(2,1)}), bf16[128,32,128]{2,1,0:T(8,128)(2,1)S(1)}, u32[]{:S(2)}, u32[]{:S(2)}) %all-to-all-start.1) | async-done | bytes 1048608 | tf_op jit(solution)/shard_map/all_to_all | solution.py:324
  215.0 1.2 collective-permute-start.17
  216.9 3.9 %all-to-all-start.2 = ((bf16[32,16,128]{2,1,0:T(8,128)(2,1)}), bf16[32,16,128]{2,1,0:T(8,128)(2,1)S(1)}, u32[]{:S(2)}, u32[]{:S(2)}) async-start(bf16[32,16,128]{2,1,0:T(8,128)(2,1)} %broadcast_in_dim.104), calls=%async_computation.2 | async-start | bytes 262144 | tf_op jit(solution)/shard_map/all_to_all | solution.py:328
  220.8 3.9 %pad_maximum_fusion.refs_2_ = bf16[384,4096]{1,0:T(8,128)(2,1)} fusion(bf16[128,4096]{1,0:T(8,128)(2,1)} %collective-permute-done.1, bf16[256,4096]{1,0:T(8,128)(2,1)} %bitcast.60), kind=kLoop, calls=%fused_computation.2 | loop fusion | flops 6291456 | bytes 6291456 | tf_op jit(solution)/shard_map/concatenate | solution.py:374
  224.7 6.9 %all_gather.7 = bf16[64,128]{1,0:T(8,128)(2,1)S(1)} all-gather(bf16[16,128]{1,0:T(8,128)(2,1)S(1)} %get-tuple-element.39), channel_id=1, replica_groups=mesh['fsdp'=4,'ctx'=32] {'fsdp'}, dimensions={0}, use_global_device_ids=true | all-gather | bytes 20480 | tf_op jit(solution)/shard_map/all_gather | solution.py:326
  232.3 1.5 collective-permute-start.19
  233.8 1.9 copy-done.1
  235.7 15.3 %project.3 = (f32[256,4096]{1,0:T(8,128)}, f32[384,4096]{1,0:T(8,128)}) custom-call(s32[4]{0:T(128)S(1)} %pad_add_fusion.refs_0_, bf16[256,4096]{1,0:T(8,128)(2,1)S(1)} %get-tuple-element.17.refs_1_, bf16[384,4096]{1,0:T(8,128)(2,1)S(1)} %copy-done.1, bf16[2048,1024]{1,0:T(8,128)(2,1)} %constant_dynamic-update-slice_fusion.5.refs_3_, ...), custom_call_target="tpu_custom_call" | custom-call | flops 5368709120 | bytes 34603008 | tf_op jit(solution)/shard_map/project/pallas_call | solution.py:278
  251.0 30.6 %project.4 = (f32[256,4096]{1,0:T(8,128)}, f32[384,4096]{1,0:T(8,128)}) custom-call(s32[4]{0:T(128)S(1)} %pad_add_fusion.refs_0_, bf16[256,4096]{1,0:T(8,128)(2,1)S(1)} %get-tuple-element.17.refs_1_, bf16[384,4096]{1,0:T(8,128)(2,1)S(1)} %copy-done.1, f32[256,4096]{1,0:T(8,128)} %get-tuple-element.18.refs_3_, ...), custom_call_target="tpu_custom_call", output_to_operand_aliasing={{0}: (3, {}), {1}: (4, {})} | custom-call | flops 10737418240 | bytes 42991616 | tf_op jit(solution)/shard_map/project/pallas_call | solution.py:278
  281.8 20.5 %project.5 = (bf16[256,4096]{1,0:T(8,128)(2,1)}, f32[384,4096]{1,0:T(8,128)}) custom-call(s32[4]{0:T(128)S(1)} %pad_add_fusion.refs_0_, bf16[256,4096]{1,0:T(8,128)(2,1)S(1)} %get-tuple-element.17.refs_1_, bf16[384,4096]{1,0:T(8,128)(2,1)} %pad_maximum_fusion.refs_2_, f32[256,4096]{1,0:T(8,128)} %get-tuple-element.20.refs_3_, ...), custom_call_target="tpu_custom_call", output_to_operand_aliasing={{1}: (4, {})} | custom-call | flops 5368709120 | bytes 34603008 | tf_op jit(solution)/shard_map/project/pallas_call | solution.py:278
  302.3 2.8 copy-done
  305.1 11.5 %backward_conv.1 = (bf16[256,4096]{1,0:T(8,128)(2,1)}, bf16[256,4096]{1,0:T(8,128)(2,1)}, bf16[256,4096]{1,0:T(8,128)(2,1)}) custom-call(f32[256,256]{1,0:T(8,128)S(1)} %pad.9.base_ref, f32[1,4096]{1,0:T(1,128)S(1)} %bitcast.59, f32[384,4096]{1,0:T(8,128)S(1)} %copy-done, f32[256,4096]{1,0:T(8,128)S(1)} %copy-done.11, bf16[256,4096]{1,0:T(8,128)(2,1)S(1)} %bitcast.57, ...), custom_call_target="tpu_custom_call" | custom-call | flops 4294967296 | bytes 25165824 | tf_op jit(solution)/shard_map/backward_conv/pallas_call | solution.py:171
  (84 shorter events, 16.2 us)
Async XLA Ops:
  4.1 8.6 %collective-permute-start.2 = (bf16[128,1024]{1,0:T(8,128)(2,1)S(1)}, bf16[128,1024]{1,0:T(8,128)(2,1)S(1)}, u32[]{:S(2)}, u32[]{:S(2)}) collective-permute-start(bf16[128,1024]{1,0:T(8,128)(2,1)S(1)} %get-tuple-element.40), channel_id=1, source_target_pairs={{0,1},{32,34},{2,3},{34,36},{4,5},{36,38},{6,7},{38,32},{8,9},{40,... | collective-permute-start | bytes 786440 | tf_op jit(solution)/shard_map/ppermute | solution.py:54
  6.6 6.2 %collective-permute-start.3 = (bf16[128,1024]{1,0:T(8,128)(2,1)S(1)}, bf16[128,1024]{1,0:T(8,128)(2,1)S(1)}, u32[]{:S(2)}, u32[]{:S(2)}) collective-permute-start(bf16[128,1024]{1,0:T(8,128)(2,1)S(1)} %get-tuple-element.40), channel_id=1, source_target_pairs={{0,65},{32,38},{2,67},{34,32},{4,69},{36,34},{6,71},{38,36},{8,73}... | collective-permute-start | bytes 786440 | tf_op jit(solution)/shard_map/ppermute | solution.py:54
  12.8 5.4 %collective-permute-start.4 = (bf16[64,1024]{1,0:T(8,128)(2,1)S(1)}, bf16[64,1024]{1,0:T(8,128)(2,1)S(1)}, u32[]{:S(2)}, u32[]{:S(2)}) collective-permute-start(bf16[64,1024]{1,0:T(8,128)(2,1)S(1)} %slice.58), channel_id=1, source_target_pairs={{0,1},{32,34},{2,3},{34,36},{4,5},{36,38},{6,7},{38,32},{8,9},{40,... | collective-permute-start | bytes 393224 | tf_op jit(solution)/shard_map/ppermute | solution.py:54
  12.9 6.0 %collective-permute-start.5 = (bf16[64,1024]{1,0:T(8,128)(2,1)S(1)}, bf16[64,1024]{1,0:T(8,128)(2,1)S(1)}, u32[]{:S(2)}, u32[]{:S(2)}) collective-permute-start(bf16[64,1024]{1,0:T(8,128)(2,1)S(1)} %slice.59), channel_id=1, source_target_pairs={{0,65},{32,38},{2,67},{34,32},{4,69},{36,34},{6,71},{38,36},{8,73}... | collective-permute-start | bytes 393224 | tf_op jit(solution)/shard_map/ppermute | solution.py:54
  19.5 15.2 %collective-permute-start.6 = (bf16[512,1024]{1,0:T(8,128)(2,1)S(1)}, bf16[512,1024]{1,0:T(8,128)(2,1)S(1)}, u32[]{:S(2)}, u32[]{:S(2)}) collective-permute-start(bf16[512,1024]{1,0:T(8,128)(2,1)S(1)} %get-tuple-element.34), channel_id=1, source_target_pairs={{0,8},{32,33},{2,10},{34,35},{4,12},{36,37},{6,14},{38,39},{8,16},... | collective-permute-start | bytes 3145736 | tf_op jit(solution)/shard_map/ppermute | solution.py:54
  20.2 14.6 %collective-permute-start.7 = (bf16[512,1024]{1,0:T(8,128)(2,1)S(1)}, bf16[512,1024]{1,0:T(8,128)(2,1)S(1)}, u32[]{:S(2)}, u32[]{:S(2)}) collective-permute-start(bf16[512,1024]{1,0:T(8,128)(2,1)S(1)} %get-tuple-element.34), channel_id=1, source_target_pairs={{0,24},{32,97},{2,26},{34,99},{4,28},{36,101},{6,30},{38,103},{8,0... | collective-permute-start | bytes 3145736 | tf_op jit(solution)/shard_map/ppermute | solution.py:54
  34.7 9.6 %collective-permute-start.8 = (bf16[256,1024]{1,0:T(8,128)(2,1)S(1)}, bf16[256,1024]{1,0:T(8,128)(2,1)S(1)}, u32[]{:S(2)}, u32[]{:S(2)}) collective-permute-start(bf16[256,1024]{1,0:T(8,128)(2,1)S(1)} %slice.60), channel_id=1, source_target_pairs={{0,8},{32,33},{2,10},{34,35},{4,12},{36,37},{6,14},{38,39},{8,16},... | collective-permute-start | bytes 1572872 | tf_op jit(solution)/shard_map/ppermute | solution.py:54
  34.8 10.3 %collective-permute-start.9 = (bf16[256,1024]{1,0:T(8,128)(2,1)S(1)}, bf16[256,1024]{1,0:T(8,128)(2,1)S(1)}, u32[]{:S(2)}, u32[]{:S(2)}) collective-permute-start(bf16[256,1024]{1,0:T(8,128)(2,1)S(1)} %slice.61), channel_id=1, source_target_pairs={{0,24},{32,97},{2,26},{34,99},{4,28},{36,101},{6,30},{38,103},{8,0... | collective-permute-start | bytes 1572872 | tf_op jit(solution)/shard_map/ppermute | solution.py:54
  37.6 11.2 %copy-start.2 = (bf16[1,256,4096]{2,1,0:T(8,128)(2,1)S(1)}, bf16[1,256,4096]{2,1,0:T(8,128)(2,1)}, u32[]{:S(2)}) copy-start(bf16[1,256,4096]{2,1,0:T(8,128)(2,1)} %param.12) | copy-start | bytes 6291460
  37.6 11.2 %copy-start.5 = (bf16[1,256,4096]{2,1,0:T(8,128)(2,1)S(1)}, bf16[1,256,4096]{2,1,0:T(8,128)(2,1)}, u32[]{:S(2)}) copy-start(bf16[1,256,4096]{2,1,0:T(8,128)(2,1)} %param.13) | copy-start | bytes 6291460
  39.6 16.8 %copy-start.15 = (bf16[1,256,4096]{2,1,0:T(8,128)(2,1)S(1)}, bf16[1,256,4096]{2,1,0:T(8,128)(2,1)}, u32[]{:S(2)}) copy-start(bf16[1,256,4096]{2,1,0:T(8,128)(2,1)} %param.14) | copy-start | bytes 6291460
  45.1 74.6 %copy-start.18 = (bf16[128,64]{0,1:T(8,128)(2,1)S(1)}, bf16[128,64]{0,1:T(8,128)(2,1)}, u32[]{:S(2)}) copy-start(bf16[128,64]{0,1:T(8,128)(2,1)} %param.20) | copy-start | bytes 49156
  46.0 83.7 %copy-start.16 = (bf16[256,128]{1,0:T(8,128)(2,1)S(1)}, bf16[256,128]{1,0:T(8,128)(2,1)}, u32[]{:S(2)}) copy-start(bf16[256,128]{1,0:T(8,128)(2,1)} %param.18) | copy-start | bytes 196612
  46.0 49.3 %collective-permute-start.11 = (bf16[2048,1024]{1,0:T(8,128)(2,1)}, bf16[2048,1024]{1,0:T(8,128)(2,1)}, u32[]{:S(2)}, u32[]{:S(2)}) collective-permute-start(bf16[2048,1024]{1,0:T(8,128)(2,1)} %constant_dynamic-update-slice_fusion.5.refs_3_), channel_id=1, source_target_pairs={{0,2},{32,40},{2,4},{34,42},{4,6},{36,44},{6,0},{38,46},{8,10},{40... | collective-permute-start | bytes 12582920 | tf_op jit(solution)/shard_map/ppermute | solution.py:54
  46.7 73.0 %collective-permute-start.13 = (bf16[2048,1024]{1,0:T(8,128)(2,1)}, bf16[2048,1024]{1,0:T(8,128)(2,1)}, u32[]{:S(2)}, u32[]{:S(2)}) collective-permute-start(bf16[2048,1024]{1,0:T(8,128)(2,1)} %constant_dynamic-update-slice_fusion.5.refs_3_), channel_id=1, source_target_pairs={{0,6},{32,56},{2,0},{34,58},{4,2},{36,60},{6,4},{38,62},{8,14},{40... | collective-permute-start | bytes 12582920 | tf_op jit(solution)/shard_map/ppermute | solution.py:54
  50.0 80.1 %copy-start.17 = (bf16[64,1024]{1,0:T(8,128)(2,1)S(1)}, bf16[64,1024]{1,0:T(8,128)(2,1)}, u32[]{:S(2)}) copy-start(bf16[64,1024]{1,0:T(8,128)(2,1)} %param.21) | copy-start | bytes 393220
  50.0 95.1 %copy-start.12 = (f32[4096]{0:T(1024)S(1)}, f32[4096]{0:T(1024)}, u32[]{:S(2)}) copy-start(f32[4096]{0:T(1024)} %param.19) | copy-start | bytes 49156
  50.0 94.1 %collective-permute-start = (bf16[128,4096]{1,0:T(8,128)(2,1)}, bf16[128,4096]{1,0:T(8,128)(2,1)S(1)}, u32[]{:S(2)}, u32[]{:S(2)}) collective-permute-start(bf16[128,4096]{1,0:T(8,128)(2,1)} %fusion.3), channel_id=1, source_target_pairs={{0,1},{1,2},{2,3},{3,4},{4,5},{5,6},{6,7},{7,8},{8,9},{9,10},{10,1... | collective-permute-start | bytes 3145736 | tf_op jit(solution)/shard_map/ppermute | solution.py:79
  51.5 180.8 %collective-permute-start.10 = (bf16[2048,1024]{1,0:T(8,128)(2,1)}, bf16[2048,1024]{1,0:T(8,128)(2,1)}, u32[]{:S(2)}, u32[]{:S(2)}) collective-permute-start(bf16[2048,1024]{1,0:T(8,128)(2,1)} %constant_dynamic-update-slice_fusion.5.refs_3_), channel_id=1, source_target_pairs={{0,32},{32,0},{2,34},{34,2},{4,36},{36,4},{6,38},{38,6},{8,40},{40... | collective-permute-start | bytes 12582920 | tf_op jit(solution)/shard_map/ppermute | solution.py:65
  57.5 112.0 %collective-permute-start.1 = (bf16[128,4096]{1,0:T(8,128)(2,1)}, bf16[128,4096]{1,0:T(8,128)(2,1)}, u32[]{:S(2)}, u32[]{:S(2)}) collective-permute-start(bf16[128,4096]{1,0:T(8,128)(2,1)} %slice_bitcast_fusion.1), channel_id=1, source_target_pairs={{1,0},{2,1},{3,2},{4,3},{5,4},{6,5},{7,6},{8,7},{9,8},{10,9},{11,1... | collective-permute-start | bytes 3145736 | tf_op jit(solution)/shard_map/ppermute | solution.py:79
  95.3 155.7 %collective-permute-start.12 = (bf16[2048,1024]{1,0:T(8,128)(2,1)}, bf16[2048,1024]{1,0:T(8,128)(2,1)}, u32[]{:S(2)}, u32[]{:S(2)}) collective-permute-start(bf16[2048,1024]{1,0:T(8,128)(2,1)} %collective-permute-done.11.refs_5_), channel_id=1, source_target_pairs={{0,32},{32,0},{2,34},{34,2},{4,36},{36,4},{6,38},{38,6},{8,40},{40... | collective-permute-start | bytes 12582920 | tf_op jit(solution)/shard_map/ppermute | solution.py:65
  119.8 131.3 %collective-permute-start.14 = (bf16[2048,1024]{1,0:T(8,128)(2,1)}, bf16[2048,1024]{1,0:T(8,128)(2,1)}, u32[]{:S(2)}, u32[]{:S(2)}) collective-permute-start(bf16[2048,1024]{1,0:T(8,128)(2,1)} %collective-permute-done.13.refs_7_), channel_id=1, source_target_pairs={{0,32},{32,0},{2,34},{34,2},{4,36},{36,4},{6,38},{38,6},{8,40},{40... | collective-permute-start | bytes 12582920 | tf_op jit(solution)/shard_map/ppermute | solution.py:65
  120.7 50.1 %all-to-all-start = ((bf16[32,64,128]{2,1,0:T(8,128)(2,1)}), bf16[32,64,128]{2,1,0:T(8,128)(2,1)}, u32[]{:S(2)}, u32[]{:S(2)}) async-start(bf16[32,64,128]{2,1,0:T(8,128)(2,1)} %broadcast_in_dim.103), calls=%async_computation | async-start | bytes 1048576 | tf_op jit(solution)/shard_map/all_to_all | solution.py:308
  144.1 1.0 copy-start.13
  145.1 1.6 copy-start.3
  146.6 1.6 copy-start.6
  148.2 1.6 copy-start.8
  149.8 1.2 copy-start.14
  160.4 9.1 %copy-start.10 = (f32[256,4096]{1,0:T(8,128)}, f32[256,4096]{1,0:T(8,128)S(1)}, u32[]{:S(2)}) copy-start(f32[256,4096]{1,0:T(8,128)S(1)} %get-tuple-element.24.gated_ref) | copy-start | bytes 12582916
  165.0 49.9 %collective-permute-start.15 = (bf16[1024,1024]{1,0:T(8,128)(2,1)}, bf16[1024,1024]{1,0:T(8,128)(2,1)}, u32[]{:S(2)}, u32[]{:S(2)}) collective-permute-start(bf16[1024,1024]{1,0:T(8,128)(2,1)} %slice.62), channel_id=1, source_target_pairs={{0,2},{32,40},{2,4},{34,42},{4,6},{36,44},{6,0},{38,46},{8,10},{40... | collective-permute-start | bytes 6291464 | tf_op jit(solution)/shard_map/ppermute | solution.py:54
  169.5 46.6 %collective-permute-start.16 = (bf16[1024,1024]{1,0:T(8,128)(2,1)}, bf16[1024,1024]{1,0:T(8,128)(2,1)}, u32[]{:S(2)}, u32[]{:S(2)}) collective-permute-start(bf16[1024,1024]{1,0:T(8,128)(2,1)} %slice.63), channel_id=1, source_target_pairs={{0,6},{32,56},{2,0},{34,58},{4,2},{36,60},{6,4},{38,62},{8,14},{40... | collective-permute-start | bytes 6291464 | tf_op jit(solution)/shard_map/ppermute | solution.py:54
  189.1 25.6 %all-to-all-start.1 = ((bf16[128,32,128]{2,1,0:T(8,128)(2,1)}), bf16[128,32,128]{2,1,0:T(8,128)(2,1)S(1)}, u32[]{:S(2)}, u32[]{:S(2)}) async-start(bf16[128,32,128]{2,1,0:T(8,128)(2,1)} %pad_maximum_fusion.1), calls=%async_computation.1 | async-start | bytes 2097152 | tf_op jit(solution)/shard_map/all_to_all | solution.py:324
  215.0 66.7 %collective-permute-start.17 = (bf16[1024,1024]{1,0:T(8,128)(2,1)}, bf16[1024,1024]{1,0:T(8,128)(2,1)}, u32[]{:S(2)}, u32[]{:S(2)}) collective-permute-start(bf16[1024,1024]{1,0:T(8,128)(2,1)} %collective-permute-done.15.refs_5_), channel_id=1, source_target_pairs={{0,32},{32,0},{2,34},{34,2},{4,36},{36,4},{6,38},{38,6},{8,40},{40... | collective-permute-start | bytes 6291464 | tf_op jit(solution)/shard_map/ppermute | solution.py:65
  216.1 65.6 %collective-permute-start.18 = (bf16[1024,1024]{1,0:T(8,128)(2,1)}, bf16[1024,1024]{1,0:T(8,128)(2,1)}, u32[]{:S(2)}, u32[]{:S(2)}) collective-permute-start(bf16[1024,1024]{1,0:T(8,128)(2,1)} %collective-permute-done.16.refs_6_), channel_id=1, source_target_pairs={{0,32},{32,0},{2,34},{34,2},{4,36},{36,4},{6,38},{38,6},{8,40},{40... | collective-permute-start | bytes 6291464 | tf_op jit(solution)/shard_map/ppermute | solution.py:65
  216.9 14.7 %all-to-all-start.2 = ((bf16[32,16,128]{2,1,0:T(8,128)(2,1)}), bf16[32,16,128]{2,1,0:T(8,128)(2,1)S(1)}, u32[]{:S(2)}, u32[]{:S(2)}) async-start(bf16[32,16,128]{2,1,0:T(8,128)(2,1)} %broadcast_in_dim.104), calls=%async_computation.2 | async-start | bytes 262144 | tf_op jit(solution)/shard_map/all_to_all | solution.py:328
  232.3 69.9 %collective-permute-start.19 = (bf16[128,4096]{1,0:T(8,128)(2,1)}, bf16[128,4096]{1,0:T(8,128)(2,1)S(1)}, u32[]{:S(2)}, u32[]{:S(2)}) collective-permute-start(bf16[128,4096]{1,0:T(8,128)(2,1)} %slice_bitcast_fusion), channel_id=1, source_target_pairs={{1,0},{2,1},{3,2},{4,3},{5,4},{6,5},{7,6},{8,7},{9,8},{10,9},{11,1... | collective-permute-start | bytes 3145736 | tf_op jit(solution)/shard_map/ppermute | solution.py:79
  233.8 1.9 copy-start.1
  281.7 20.5 %copy-start.4 = (bf16[1,256,4096]{2,1,0:T(8,128)(2,1)S(1)}, bf16[1,256,4096]{2,1,0:T(8,128)(2,1)}, u32[]{:S(2)}) copy-start(bf16[1,256,4096]{2,1,0:T(8,128)(2,1)} %param.12) | copy-start | bytes 6291460
  281.7 20.5 %copy-start.7 = (bf16[1,256,4096]{2,1,0:T(8,128)(2,1)S(1)}, bf16[1,256,4096]{2,1,0:T(8,128)(2,1)}, u32[]{:S(2)}) copy-start(bf16[1,256,4096]{2,1,0:T(8,128)(2,1)} %param.13) | copy-start | bytes 6291460
  281.7 20.5 %copy-start.9 = (bf16[1,256,4096]{2,1,0:T(8,128)(2,1)S(1)}, bf16[1,256,4096]{2,1,0:T(8,128)(2,1)}, u32[]{:S(2)}) copy-start(bf16[1,256,4096]{2,1,0:T(8,128)(2,1)} %param.11) | copy-start | bytes 6291460
  281.7 20.5 %copy-start.11 = (f32[256,4096]{1,0:T(8,128)S(1)}, f32[256,4096]{1,0:T(8,128)}, u32[]{:S(2)}) copy-start(f32[256,4096]{1,0:T(8,128)} %copy-done.10) | copy-start | bytes 12582916
  302.3 2.8 copy-start

commit v2 on v1

v2 whole, which is shorter than its diff:
```python
import functools
import math

import jax
import jax.numpy as jnp
from jax import lax
from jax.experimental import pallas as pl
from jax.experimental.pallas import tpu as pltpu
from jax.sharding import PartitionSpec as P

QBLOCK = 64
BOTH = ("fsdp", "ctx")
RING = (0, 3, 1, 2)

normal_levels = (
    -1.0,
    -0.6961928009986877,
    -0.5250730514526367,
    -0.39491748809814453,
    -0.28444138169288635,
    -0.18477343022823334,
    -0.09105003625154495,
    0.0,
    0.07958029955625534,
    0.16093020141124725,
    0.24611230194568634,
    0.33791524171829224,
    0.44070982933044434,
    0.5626170039176941,
    0.7229568362236023,
    1.0,
)
adapter_scale = 0.25


def device_index(x, y, z, c):
    return ((x // 2) * 2 + c) * 32 + y * 8 + z * 2 + x % 2


def ring_pairs(axis0, axis1, step):
    pairs = []
    for x in range(4):
        for y in range(4):
            for z in range(4):
                for c in range(2):
                    to = [x, y, z]
                    axis = (axis0, axis1)[c]
                    to[axis] = (to[axis] + step) % 4
                    pairs.append((device_index(x, y, z, c), device_index(*to, c)))
    return pairs


def send(block, axis0, axis1, step):
    return lax.ppermute(block, BOTH, ring_pairs(axis0, axis1, step))


def swap_cores(block):
    pairs = [
        (device_index(x, y, z, c), device_index(x, y, z, 1 - c))
        for x in range(4)
        for y in range(4)
        for z in range(4)
        for c in range(2)
    ]
    return lax.ppermute(block, BOTH, pairs)


def ring_phase(block, axis0, axis1):
    half = block.shape[0] // 2
    plus = send(block, axis0, axis1, 1)
    minus = send(block, axis0, axis1, -1)
    far_low = send(plus[:half], axis0, axis1, 1)
    far_high = send(minus[half:], axis0, axis1, -1)
    return plus, minus, far_low, far_high


def after(block, *earlier):
    return lax.optimization_barrier((block, earlier))[0]


def along_ctx(shard, by):
    pairs = [(i, i + by) for i in range(32) if 0 <= i + by < 32]
    return lax.ppermute(shard, "ctx", pairs)


def next_rows(block, ctx):
    xl, z = ctx % 2, (ctx // 2) % 4
    along_y = [(i, i + 8) for i in range(32) if i % 8 == 7 and i + 8 < 32]
    relayed = lax.ppermute(block, "ctx", along_y)
    along_z = [
        (i, i + 2 if i % 8 != 7 else i - 6) for i in range(32) if i % 2 == 1 and (i % 8 != 7 or i >= 15)
    ]
    block_z = jnp.where(z == 3, relayed, block)
    relayed = lax.ppermute(block_z, "ctx", along_z)
    return relayed


def pair_rows(block, relayed, ctx):
    crossed = lax.ppermute(
        jnp.where(ctx % 2 == 0, block, relayed), "ctx", [(i, i ^ 1) for i in range(32)]
    )
    return jnp.where(ctx == 0, jnp.zeros_like(crossed), crossed)


def weight_piece(codes, scale_bytes, row_scale, down, up):
    levels = jnp.zeros(codes.shape, jnp.float32)
    for number in range(16):
        levels = jnp.where(codes == number, normal_levels[number], levels)
    absmax = row_scale[:, None] * (scale_bytes.astype(jnp.float32) + 1.0) / 256.0
    absmax = jnp.repeat(absmax, QBLOCK, axis=1)
    weight = (levels * absmax).astype(jnp.bfloat16).astype(jnp.float32)
    low_rank = jnp.dot(down, up, preferred_element_type=jnp.float32)
    return (weight + adapter_scale * low_rank).astype(jnp.bfloat16)


def toeplitz_conv(base, window, width):
    lane = lax.broadcasted_iota(jnp.int32, (128, 2 * width), 1)
    group_of = (lane % width) // 16
    total = None
    for group in range(width // 16):
        row = jnp.broadcast_to(base[group : group + 1, :], (128, 256))
        toep = pltpu.roll(row, 0, 1, stride=1, stride_axis=0).astype(jnp.bfloat16)
        part = jnp.dot(toep, window, preferred_element_type=jnp.float32)
        total = part if total is None else jnp.where(group_of == group, part, total)
    return total


def forward_kernel(base_ref, skip_ref, query_ref, key_ref, value_ref, halo_ref, gated_ref, signal_ref, *, tiles):
    for tile in range(tiles):
        lanes = pl.ds(tile * 128, 128)
        mixed = (
            key_ref[:, lanes].astype(jnp.float32) * value_ref[:, lanes].astype(jnp.float32)
        ).astype(jnp.bfloat16)
        first = jnp.concatenate([halo_ref[:, lanes], mixed[:128]], 0)
        window = jnp.concatenate([first, mixed], 1)
        conv = toeplitz_conv(base_ref[pl.ds(tile * 8, 8), :], window, 128)
        conv = jnp.concatenate([conv[:, :128], conv[:, 128:]], 0)
        gated = conv + skip_ref[:, lanes] * mixed.astype(jnp.float32)
        gated_ref[:, lanes] = gated
        signal_ref[:, lanes] = (query_ref[:, lanes].astype(jnp.float32) * gated).astype(jnp.bfloat16)


def forward_conv(base, skip, query, key, value, halo):
    rows, channels = query.shape
    width = 512
    block = pl.BlockSpec((rows, width), lambda j: (0, j))
    return pl.pallas_call(
        functools.partial(forward_kernel, tiles=width // 128),
        grid=(channels // width,),
        in_specs=[
            pl.BlockSpec((width // 16, 256), lambda j: (j, 0)),
            pl.BlockSpec((1, width), lambda j: (0, j)),
            block,
            block,
            block,
            pl.BlockSpec((128, width), lambda j: (0, j)),
        ],
        out_specs=[block, block],
        out_shape=[
            jax.ShapeDtypeStruct((rows, channels), jnp.float32),
            jax.ShapeDtypeStruct((rows, channels), jnp.bfloat16),
        ],
        compiler_params=pltpu.CompilerParams(vmem_limit_bytes=54 << 20),
        cost_estimate=pl.CostEstimate(flops=1 << 32, bytes_accessed=14 << 20, transcendentals=0),
        name="forward_conv",
    )(base, skip, query, key, value, halo)


def backward_kernel(
    base_ref, skip_ref, head_ref, tail_ref, halo_ref, key_ref, value_ref, *refs, tiles
):
    grad_key_ref, grad_value_ref = refs[-2:]
    for tile in range(tiles):
        lanes = pl.ds(tile * 128, 128)
        here = jnp.concatenate([head_ref[:, lanes], tail_ref[:, lanes]], 0)
        second = jnp.concatenate([tail_ref[:, lanes], halo_ref[:, lanes]], 0)
        window = jnp.concatenate([here, second], 1)
        conv = toeplitz_conv(base_ref[pl.ds(tile * 8, 8), :], window, 128)
        conv = jnp.concatenate([conv[:, :128], conv[:, 128:]], 0)
        mixed = conv + skip_ref[:, lanes] * here.astype(jnp.float32)
        grad_key_ref[:, lanes] = (mixed * value_ref[:, lanes].astype(jnp.float32)).astype(jnp.bfloat16)
        grad_value_ref[:, lanes] = (mixed * key_ref[:, lanes].astype(jnp.float32)).astype(jnp.bfloat16)


def backward_conv(base, skip, head, tail, halo, key, value, part, results):
    rows, channels = key.shape
    width = 512
    skipped = part * (channels // 2 // width)
    block = pl.BlockSpec((rows, width), lambda j: (0, j + skipped))
    half = pl.BlockSpec((128, width), lambda j: (0, j))
    anywhere = pl.BlockSpec(memory_space=pl.ANY)
    return pl.pallas_call(
        functools.partial(backward_kernel, tiles=width // 128),
        grid=(channels // 2 // width,),
        in_specs=[
            pl.BlockSpec((width // 16, 256), lambda j: (j + skipped, 0)),
            pl.BlockSpec((1, width), lambda j: (0, j + skipped)),
            half,
            pl.BlockSpec((128, width), lambda j: (0, j + skipped)),
            half,
            block,
            block,
        ]
        + [anywhere] * len(results),
        out_specs=[block] * 2,
        out_shape=[jax.ShapeDtypeStruct((rows, channels), jnp.bfloat16)] * 2,
        input_output_aliases={7: 0, 8: 1} if results else {},
        compiler_params=pltpu.CompilerParams(vmem_limit_bytes=54 << 20),
        cost_estimate=pl.CostEstimate(flops=1 << 31, bytes_accessed=6 << 20, transcendentals=0),
        name="backward_conv",
    )(base, skip, head, tail, halo, key, value, *results)


def project_kernel(*refs, groups, first, last):
    refs = list(refs)
    meta = refs.pop(0)
    signal_ref, cot_ref = refs.pop(0), refs.pop(0)
    if not first:
        out_in, back_in = refs.pop(0), refs.pop(0)
    arrays = [[refs.pop(0) for _ in range(count)] for _, _, count in groups]
    if last:
        gated_ref, query_ref, out_ref, grad_query_ref, *head_refs = refs[:6]
        tail_ref, refs = refs[6], refs[7:]
    else:
        out_ref, back_ref = refs[:2]
        refs = refs[2:]
    signal, picked, cot, out_acc, back_acc, held, sems, io_sems = refs[:8]
    x0, y0, z0, core = meta[0], meta[1], meta[2], meta[3]
    rows = signal.shape[0]
    loads = [
        pltpu.make_async_copy(signal_ref, signal, io_sems.at[0]),
        pltpu.make_async_copy(cot_ref, cot, io_sems.at[1]),
    ]
    if not first:
        loads.append(pltpu.make_async_copy(out_in, out_acc, io_sems.at[3]))
        loads.append(pltpu.make_async_copy(back_in, back_acc, io_sems.at[4]))
    for load in loads:
        load.start()
    copies = []
    for g, (mine, _, count) in enumerate(groups):
        chain = core if mine else 1 - core
        each = 16 // count
        group = []
        for n in range(16):
            a, b = RING[n // 4], RING[n % 4]
            x = (x0 + jnp.where(chain == 0, b, a)) & 3
            w = jnp.where(chain == 0, y0 + a, z0 + b) & 3
            slot = pl.multiple_of(((x >> 1) * 8 + w * 2 + (x & 1)) * 128, 128)
            source = arrays[g][n // each].at[pl.ds((n % each) * 128, 128), :]
            group.append(
                pltpu.make_async_copy(source, held.at[g, pl.ds(slot, 128), :], sems.at[g, n])
            )
        copies.append(group)
    for group in copies[:2]:
        for copy in group:
            copy.start()
    late = []
    if last:
        gated, query, gradient = refs[8:11]
        for n, (source, target) in enumerate([(gated_ref, gated), (query_ref, query)]):
            late.append(pltpu.make_async_copy(source, target, io_sems.at[5 + n]))
    if first:
        out_acc[...] = jnp.zeros_like(out_acc)
        back_acc[...] = jnp.zeros_like(back_acc)
    for load in loads:
        load.wait()
    for g, (mine, offset, _) in enumerate(groups):
        chain = core if mine else 1 - core
        fixed = jnp.where(chain == 0, z0 + offset, y0 + offset) & 3

        def channels(w, chain=chain, fixed=fixed):
            return pl.multiple_of(jnp.where(chain == 0, w * 4 + fixed, fixed * 4 + w) * 256, 256)

        for w in range(4):
            picked[:, w * 256 : (w + 1) * 256] = signal[:, pl.ds(channels(w), 256)]
        for copy in copies[g]:
            copy.wait()
        for copy in copies[g + 2] if g + 2 < len(groups) else late if g == 0 else ():
            copy.start()

        @pl.loop(0, 2)
        def _(xh, g=g, chain=chain, channels=channels):
            cols = pl.ds(pl.multiple_of((xh * 2 + chain) * 1024, 1024), 1024)
            weight = held.at[g, pl.ds(pl.multiple_of(xh * 1024, 1024), 1024), :]
            out_acc[:, cols] += jnp.dot(picked[...], weight[...], preferred_element_type=jnp.float32)
            back = lax.dot_general(
                cot[:, cols], weight[...], (((1,), (1,)), ((), ())), preferred_element_type=jnp.float32
            )
            for w in range(4):
                back_acc[:, pl.ds(channels(w), 256)] += back[:, w * 256 : (w + 1) * 256]

    if not last:
        stores = [
            pltpu.make_async_copy(out_acc, out_ref, io_sems.at[0]),
            pltpu.make_async_copy(back_acc, back_ref, io_sems.at[1]),
        ]
        for store in stores:
            store.start()
        for store in stores:
            store.wait()
        return
    signal[...] = out_acc[...].astype(jnp.bfloat16)
    stores = [pltpu.make_async_copy(signal, out_ref, io_sems.at[0])]
    stores[0].start()
    for load in late:
        load.wait()
    for quarter in range(4):

        @pl.loop(0, 4)
        def _(step, quarter=quarter):
            lanes = pl.ds(pl.multiple_of(quarter * 1024 + step * 256, 256), 256)
            back = back_acc[:, lanes]
            gradient[:, lanes] = (back * query[:, lanes].astype(jnp.float32)).astype(jnp.bfloat16)
            query[:, lanes] = (back * gated[:, lanes]).astype(jnp.bfloat16)

        part = pl.ds(quarter * 1024, 1024)
        head = head_refs[quarter // 2].at[:, pl.ds((quarter % 2) * 1024, 1024)]
        for n, (source, target) in enumerate(
            [
                (gradient.at[pl.ds(0, 128), part], head),
                (gradient.at[pl.ds(128, 128), part], tail_ref.at[:, part]),
                (query.at[:, part], grad_query_ref.at[:, part]),
            ]
        ):
            stores.append(pltpu.make_async_copy(source, target, sems.at[0, quarter * 3 + n]))
            stores[-1].start()
    for store in stores:
        store.wait()


def project(meta, signal, cot, sums, groups, finish=None):
    rows, channels = signal.shape
    first, last = sums is None, finish is not None
    arrays = [array for group in groups for array in group[2]]
    static = tuple((mine, offset, len(held)) for mine, offset, held in groups)
    anywhere = pl.BlockSpec(memory_space=pl.ANY)
    operands = [meta, signal, cot] + ([] if first else list(sums)) + arrays
    in_specs = [pl.BlockSpec(memory_space=pltpu.SMEM)] + [anywhere] * (len(operands) - 1)
    flops = len(groups) * 16 * 128 * 1024 * 2 * rows * 2
    moved = len(groups) * (4 << 20) + (16 << 20)
    scratch = [
        pltpu.VMEM((rows, channels), jnp.bfloat16),
        pltpu.VMEM((rows, 1024), jnp.bfloat16),
        pltpu.VMEM((rows, channels), jnp.bfloat16),
        pltpu.VMEM((rows, channels), jnp.float32),
        pltpu.VMEM((rows, channels), jnp.float32),
        pltpu.VMEM((len(groups), 2048, 1024), jnp.bfloat16),
        pltpu.SemaphoreType.DMA((len(groups), 16)),
        pltpu.SemaphoreType.DMA((10,)),
    ]
    if last:
        operands += list(finish)
        in_specs += [anywhere] * 2
        out_shape = [jax.ShapeDtypeStruct((rows, channels), jnp.bfloat16)] * 2
        out_shape += [jax.ShapeDtypeStruct((128, channels // 2), jnp.bfloat16)] * 2
        out_shape += [jax.ShapeDtypeStruct((128, channels), jnp.bfloat16)]
        scratch += [
            pltpu.VMEM((rows, channels), jnp.float32),
            pltpu.VMEM((rows, channels), jnp.bfloat16),
            pltpu.VMEM((rows, channels), jnp.bfloat16),
        ]
        aliases = {}
    else:
        out_shape = [
            jax.ShapeDtypeStruct((rows, channels), jnp.float32),
            jax.ShapeDtypeStruct((rows, channels), jnp.float32),
        ]
        aliases = {} if first else {3: 0, 4: 1}
    return pl.pallas_call(
        functools.partial(project_kernel, groups=static, first=first, last=last),
        in_specs=in_specs,
        out_specs=[anywhere] * len(out_shape),
        out_shape=out_shape,
        scratch_shapes=scratch,
        input_output_aliases=aliases,
        compiler_params=pltpu.CompilerParams(vmem_limit_bytes=54 << 20),
        cost_estimate=pl.CostEstimate(flops=flops, bytes_accessed=moved, transcendentals=0),
        name="project",
    )(*operands)


def gathered_adapters(down_piece, up_piece, ctx, fsdp):
    quarter = lax.dynamic_slice_in_dim(down_piece.T, fsdp * 16, 16, 0)
    block = lax.dynamic_slice(up_piece, ((ctx // 4) * 8, (ctx % 4) * 256), (8, 256))
    block = jnp.concatenate([block[:, :128], block[:, 128:]], 0)
    share = jnp.concatenate([quarter, block], 0)
    shares = lax.all_to_all(jnp.broadcast_to(share[None], (128, 32, 128)), BOTH, 0, 0, tiled=True)
    return shares


def adapter_kernel(signal_ref, cot_ref, shares_ref, parts_ref, down_ref, up_ref):
    for d in range(128):
        fsdp, ctx = d // 32, d % 32
        down_ref[fsdp * 16 : fsdp * 16 + 16, ctx * 128 : ctx * 128 + 128] = shares_ref[d, 0:16, :]
        top, left = (ctx // 4) * 8, fsdp * 1024 + (ctx % 4) * 256
        up_ref[top : top + 8, left : left + 128] = shares_ref[d, 16:24, :]
        up_ref[top : top + 8, left + 128 : left + 256] = shares_ref[d, 24:32, :]
    across = (((1,), (1,)), ((), ()))
    over_rows = (((0,), (0,)), ((), ()))
    down_projection = lax.dot_general(
        signal_ref[...], down_ref[...], across, preferred_element_type=jnp.float32
    ).astype(jnp.bfloat16)
    back_up = lax.dot_general(
        cot_ref[...], up_ref[...], across, preferred_element_type=jnp.float32
    ).astype(jnp.bfloat16)
    down_ref[...] = lax.dot_general(
        back_up, signal_ref[...], over_rows, preferred_element_type=jnp.float32
    ).astype(jnp.bfloat16)
    up_ref[...] = lax.dot_general(
        down_projection, cot_ref[...], over_rows, preferred_element_type=jnp.float32
    ).astype(jnp.bfloat16)
    for d in range(128):
        fsdp, ctx = d // 32, d % 32
        parts_ref[d, 0:16, :] = down_ref[fsdp * 16 : fsdp * 16 + 16, ctx * 128 : ctx * 128 + 128]
        top, left = (ctx // 4) * 8, fsdp * 1024 + (ctx % 4) * 256
        parts_ref[d, 16:24, :] = up_ref[top : top + 8, left : left + 128]
        parts_ref[d, 24:32, :] = up_ref[top : top + 8, left + 128 : left + 256]


def adapter_terms(signal, cot, shares):
    return pl.pallas_call(
        adapter_kernel,
        out_shape=jax.ShapeDtypeStruct((128, 32, 128), jnp.bfloat16),
        scratch_shapes=[pltpu.VMEM((64, 4096), jnp.bfloat16)] * 2,
        compiler_params=pltpu.CompilerParams(vmem_limit_bytes=54 << 20),
        cost_estimate=pl.CostEstimate(flops=1 << 32, bytes_accessed=6 << 20, transcendentals=0),
        name="adapter_terms",
    )(signal, cot, shares)


def adapter_results(parts, multiplier):
    sums = (multiplier * jnp.sum(parts.astype(jnp.float32), 0)).astype(jnp.bfloat16)
    grad_down = lax.all_gather(sums[:16], "fsdp", axis=0, tiled=True)
    up = lax.all_to_all(jnp.broadcast_to(sums[None, 16:], (32, 16, 128)), "ctx", 0, 0, tiled=True)
    grad_up = jnp.transpose(up.reshape(8, 4, 2, 8, 128), (0, 3, 1, 2, 4)).reshape(64, 1024)
    return grad_down.T, grad_up


def local(
    query_branch,
    key_branch,
    value_branch,
    cotangent,
    quantized_weight_codes,
    scale_code_bytes,
    row_scale_second,
    filters,
    channel_skip_weight,
    adapter_down_weight,
    adapter_up_weight,
):
    query, key, value, cot = query_branch[0], key_branch[0], value_branch[0], cotangent[0]
    rows, channels = query.shape
    multiplier = adapter_scale / math.sqrt(4 * 8192)
    ctx, fsdp = lax.axis_index("ctx"), lax.axis_index("fsdp")
    core = fsdp % 2
    meta = jnp.stack([(fsdp // 2) * 2 + ctx % 2, ctx // 8, (ctx // 2) % 4, core]).astype(jnp.int32)

    piece = weight_piece(
        quantized_weight_codes, scale_code_bytes, row_scale_second, adapter_down_weight, adapter_up_weight
    )
    mixed_tail = (key[128:].astype(jnp.float32) * value[128:].astype(jnp.float32)).astype(jnp.bfloat16)
    relayed = next_rows(mixed_tail, ctx)
    plus, minus, low, high = ring_phase(piece, 0, 2)
    held = jnp.concatenate([piece, plus, minus, low, high], 0)
    shares = gathered_adapters(after(adapter_down_weight, held), adapter_up_weight, ctx, fsdp)
    plus, minus, low, high = ring_phase(held, 1, 0)
    front = jnp.concatenate([held, plus], 0)
    rear = after(jnp.concatenate([minus, low, high], 0), front, relayed, shares)
    mixed_halo = pair_rows(mixed_tail, after(relayed, rear), ctx)
    plus_front, minus_front = send(front, 2, 1, 1), send(front, 2, 1, -1)
    plus_rear, minus_rear = send(rear, 2, 1, 1), send(rear, 2, 1, -1)

    taps = filters.astype(jnp.float32)
    forward_base = jnp.pad(jnp.flip(taps, 1), ((0, 0), (1, 127)))
    backward_base = jnp.pad(taps, ((0, 0), (0, 128)))
    skip = channel_skip_weight[None]
    gated, signal = forward_conv(forward_base, skip, query, key, after(value, rear), mixed_halo)

    far_front = send(after(plus_front, signal), 2, 1, 1)
    far_rear = send(minus_rear, 2, 1, -1)
    terms = adapter_terms(signal, cot, shares)
    parts = lax.all_to_all(terms, BOTH, 0, 0, tiled=True)
    swapped = [
        swap_cores(after(block, signal))
        for block in (front, rear, plus_front, plus_rear, minus_front, minus_rear)
    ]
    sums = project(
        meta,
        after(signal, terms),
        cot,
        None,
        [
            (True, 0, [front, rear]),
            (False, 0, swapped[:2]),
            (True, -1, [plus_front, plus_rear]),
            (False, -1, swapped[2:4]),
            (True, 1, [minus_front, minus_rear]),
            (False, 1, swapped[4:]),
        ],
    )
    far = [swap_cores(after(block, sums[0])) for block in (far_front, far_rear)]
    output, grad_query, head_a, head_b, tail = project(
        meta,
        signal,
        cot,
        sums,
        [(True, 2, [far_front, far_rear]), (False, 2, far)],
        (gated, query),
    )
    halo_a, halo_b = along_ctx(head_a, -1), along_ctx(head_b, -1)
    grad_down, grad_up = adapter_results(after(parts, output), multiplier)
    results = backward_conv(backward_base, skip, head_a, tail, halo_a, key, value, 0, ())
    grad_key, grad_value = backward_conv(
        backward_base, skip, head_b, tail, halo_b, key, value, 1, tuple(results)
    )
    return output[None], grad_query[None], grad_key[None], grad_value[None], grad_down, grad_up


def solution(mesh):
    return jax.shard_map(
        local,
        mesh=mesh,
        in_specs=(
            P("fsdp", "ctx", None),
            P("fsdp", "ctx", None),
            P("fsdp", "ctx", None),
            P("fsdp", "ctx", None),
            P("ctx", "fsdp"),
            P("ctx", "fsdp"),
            P("ctx"),
            P(),
            P(),
            P("ctx", None),
            P(None, "fsdp"),
        ),
        out_specs=(
            P("fsdp", "ctx", None),
            P("fsdp", "ctx", None),
            P("fsdp", "ctx", None),
            P("fsdp", "ctx", None),
            P("ctx", None),
            P(None, "fsdp"),
        ),
        check_vma=False,
    )
```

time: 322 us -> 245 us (0.76)
  local copies, waits for them, and re-layouts: 40.8 us -> 14.5 us
  blocking collectives: 20.9 us -> 7.67 us
  Pallas kernels: 87.3 us -> 74.6 us
  waiting for transfers between devices: 75.7 us -> 63.6 us
  matrix products: 10.8 us -> 2.47 us
    ppermute x5 -> x8, starting transfers between devices: 30.7 us -> 2.57 us  [swap_cores(): return lax.ppermute(block, BOTH, pairs)]
    ppermute x12 -> x14, waiting for transfers between devices: 58.7 us -> 34.9 us  [send(): return lax.ppermute(block, BOTH, ring_pairs(axis0, axis1, step))]
    pallas_call x3 -> x2, Pallas kernels: 66.4 us -> 43.4 us  [project(): pl.pallas_call(functools.partial(project_kernel, groups=static, first=fir...]
    ppermute x0 -> x3, waiting for transfers between devices: none -> 16.1 us  [the longest x1 16.1 us: pair_rows(): lax.ppermute(jnp.where(ctx % 2 == 0, block, relayed), 'ctx', [(i, i ^ 1)...]
    all_to_all x3, starting transfers between devices: 19 us -> 32.4 us  [the longest x1 16.2 us: gathered_adapters(): lax.all_to_all(jnp.broadcast_to(share[None], (128, 32, 128)), BOTH, 0, 0,...]
    all_gather x2 -> x1, blocking collectives: 20.9 us -> 7.67 us  [adapter_results(): grad_down = lax.all_gather(sums[:16], 'fsdp', axis=0, tiled=True)]
    unnamed x46 -> x38, local copies, waits for them, and re-layouts: 18.5 us -> 8.06 us
    dot_general x2 -> x0, matrix products: 8.23 us -> none  [the longest x1 4.2 us: adapter_gradients(): lax.dot_general(down_projection, cot, over_rows, preferred_element_type=j...]
  transfers between devices with their start and end apart: 23 -> 30, of which waited for: 6 -> 8; matrix products, arithmetic and copies ran while one was open for 13% -> 7% of each run, Pallas kernels for 24% -> 28%
where the time goes in v2:
time: 245 us; the launch traced here: 242 us
  Pallas kernels  74.6 us (30%)
  starting transfers between devices  69.1 us (28%)
  waiting for transfers between devices  63.6 us (26%)
  local copies, waits for them, and re-layouts  14.5 us (6%)
  other arithmetic  8.59 us (4%)
  blocking collectives  7.67 us (3%)
  matrix products  2.47 us (1%)
    pallas_call x2, Pallas kernels, project(): pl.pallas_call(functools.partial(project_kernel, groups=static, first=fir...  43.4 us
    ppermute x14, waiting for transfers between devices, send(): return lax.ppermute(block, BOTH, ring_pairs(axis0, axis1, step))  34.9 us
    ppermute x14, starting transfers between devices, send(): return lax.ppermute(block, BOTH, ring_pairs(axis0, axis1, step))  23.5 us
    all_to_all x1, starting transfers between devices, gathered_adapters(): lax.all_to_all(jnp.broadcast_to(share[None], (128, 32, 128)), BOTH, 0, 0,...  16.2 us
    ppermute x1, waiting for transfers between devices, pair_rows(): lax.ppermute(jnp.where(ctx % 2 == 0, block, relayed), 'ctx', [(i, i ^ 1)...  16.1 us
    pallas_call x2, Pallas kernels, backward_conv(): pl.pallas_call(functools.partial(backward_kernel, tiles=width // 128), gr...  13.5 us
    pallas_call x1, Pallas kernels, forward_conv(): pl.pallas_call(functools.partial(forward_kernel, tiles=width // 128), gri...  12 us
    all_to_all x1, waiting for transfers between devices, adapter_results(): lax.all_to_all(jnp.broadcast_to(sums[None, 16:], (32, 16, 128)), 'ctx', 0...  10.1 us
  transfers between devices with their start and end apart: 30, of which 8 were waited for; matrix products, arithmetic and copies ran while one was open for 7% of the time, Pallas kernels for 28%

profile of v2, /device:TPU:1, one launch (start us, length us, event | category | flops | bytes accessed | tf_op | source)
XLA Modules:
  0.0 241.6 jit_solution(8400540659072936991)
XLA Ops:
  0.7 1.8 fusion.2
  2.5 1.7 collective-permute-start.8
  4.5 2.5 %constant_dynamic-update-slice_fusion.10 = (bf16[1024,1024]{1,0:T(8,128)(2,1)}, bf16[512,1024]{1,0:T(8,128)(2,1)S(1)}, bf16[128,1024]{1,0:T(8,128)(2,1)S(1)}) fusion(bf16[128,64]{0,1:T(8,128)(2,1)S(1)} %copy-done, bf16[64,1024]{1,0:T(8,128)(2,1)S(1)} %copy-done.8, f32[128,1024]{1,0:T(8,128)S(1)} %copy.20, s32[128,1024]{1,0:T(8,128)} %param.15), kind=kOutput, calls=%fused_computation.21 | convolution fusion | flops 21757952 | bytes 1982464 | tf_op jit(solution)/shard_map/dot_general | solution.py:112
  7.0 2.5 %collective-permute-start = (bf16[128,1024]{1,0:T(8,128)(2,1)S(1)}, bf16[128,1024]{1,0:T(8,128)(2,1)S(1)}, u32[]{:S(2)}, u32[]{:S(2)}) collective-permute-start(bf16[128,1024]{1,0:T(8,128)(2,1)S(1)} %get-tuple-element.74), channel_id=1, source_target_pairs={{0,1},{32,34},{2,3},{34,36},{4,5},{36,38},{6,7},{38,32},{8,9},{40,... | collective-permute-start | bytes 786440 | tf_op jit(solution)/shard_map/ppermute | solution.py:54
  9.4 2.1 collective-permute-start.1
  11.6 4.0 %collective-permute-done = bf16[128,1024]{1,0:T(8,128)(2,1)S(1)} collective-permute-done((bf16[128,1024]{1,0:T(8,128)(2,1)S(1)}, bf16[128,1024]{1,0:T(8,128)(2,1)S(1)}, u32[]{:S(2)}, u32[]{:S(2)}) %collective-permute-start) | collective-permute-done | bytes 262176 | tf_op jit(solution)/shard_map/ppermute | solution.py:54
  15.7 2.7 %collective-permute-start.3 = (bf16[64,1024]{1,0:T(8,128)(2,1)S(1)}, bf16[64,1024]{1,0:T(8,128)(2,1)S(1)}, u32[]{:S(2)}, u32[]{:S(2)}) collective-permute-start(bf16[64,1024]{1,0:T(8,128)(2,1)S(1)} %slice.43), channel_id=1, source_target_pairs={{0,65},{32,38},{2,67},{34,32},{4,69},{36,34},{6,71},{38,36},{8,73}... | collective-permute-start | bytes 393224 | tf_op jit(solution)/shard_map/ppermute | solution.py:54
  20.0 1.0 collective-permute-done.2
  22.4 1.0 copy-done.14
  23.3 3.2 %collective-permute-start.5 = (bf16[512,1024]{1,0:T(8,128)(2,1)}, bf16[512,1024]{1,0:T(8,128)(2,1)S(1)}, u32[]{:S(2)}, u32[]{:S(2)}) collective-permute-start(bf16[512,1024]{1,0:T(8,128)(2,1)} %copy-done.14), channel_id=1, source_target_pairs={{0,8},{32,33},{2,10},{34,35},{4,12},{36,37},{6,14},{38,39},{8,16},... | collective-permute-start | bytes 3145736 | tf_op jit(solution)/shard_map/ppermute | solution.py:54
  26.5 1.3 collective-permute-start.4
  27.8 1.1 broadcast_select_fusion.2
  28.9 1.7 collective-permute-start.9
  30.6 1.1 broadcast_in_dim.102
  31.7 16.2 %all-to-all-start = ((bf16[128,32,128]{2,1,0:T(8,128)(2,1)}), bf16[128,32,128]{2,1,0:T(8,128)(2,1)}, u32[]{:S(2)}, u32[]{:S(2)}) async-start(bf16[128,32,128]{2,1,0:T(8,128)(2,1)} %broadcast_in_dim.102), calls=%async_computation | async-start | bytes 2097152 | tf_op jit(solution)/shard_map/all_to_all | solution.py:387
  47.9 0.8 slice.44
  48.8 1.4 collective-permute-start.6
  50.1 0.8 slice.45
  51.0 1.3 collective-permute-start.7
  52.3 1.0 constant_dynamic-update-slice_fusion.5.refs_3_
  53.3 14.3 %collective-permute-done.6 = bf16[256,1024]{1,0:T(8,128)(2,1)} collective-permute-done((bf16[256,1024]{1,0:T(8,128)(2,1)}, bf16[256,1024]{1,0:T(8,128)(2,1)}, u32[]{:S(2)}, u32[]{:S(2)}) %collective-permute-start.6) | collective-permute-done | bytes 524320 | tf_op jit(solution)/shard_map/ppermute | solution.py:54
  67.6 2.7 %pad_maximum_fusion.refs_4_ = bf16[1024,1024]{1,0:T(8,128)(2,1)} fusion(bf16[256,1024]{1,0:T(8,128)(2,1)} %collective-permute-done.7, bf16[256,1024]{1,0:T(8,128)(2,1)} %collective-permute-done.6, bf16[512,1024]{1,0:T(8,128)(2,1)S(1)} %collective-permute-done.4), kind=kLoop, calls=%fused_computation | loop fusion | flops 6291456 | bytes 4194304 | tf_op jit(solution)/shard_map/concatenate | solution.py:469
  70.3 1.1 broadcast_select_fusion
  71.4 4.7 %collective-permute-start.10 = (bf16[128,4096]{1,0:T(8,128)(2,1)}, bf16[128,4096]{1,0:T(8,128)(2,1)S(1)}, u32[]{:S(2)}, u32[]{:S(2)}) collective-permute-start(bf16[128,4096]{1,0:T(8,128)(2,1)} %broadcast_select_fusion), channel_id=1, source_target_pairs={{0,1},{1,0},{2,3},{3,2},{4,5},{5,4},{6,7},{7,6},{8,9},{9,8},{10,11... | collective-permute-start | bytes 3145736 | tf_op jit(solution)/shard_map/ppermute | solution.py:99
  76.3 0.8 pad.8.base_ref
  77.1 3.7 %collective-permute-start.17 = (bf16[1024,1024]{1,0:T(8,128)(2,1)}, bf16[1024,1024]{1,0:T(8,128)(2,1)S(1)}, u32[]{:S(2)}, u32[]{:S(2)}) collective-permute-start(bf16[1024,1024]{1,0:T(8,128)(2,1)} %constant_dynamic-update-slice_fusion.5.refs_3_), channel_id=1, source_target_pairs={{0,6},{32,56},{2,0},{34,58},{4,2},{36,60},{6,4},{38,62},{8,14},{40... | collective-permute-start | bytes 6291464 | tf_op jit(solution)/shard_map/ppermute | solution.py:54
  80.9 2.7 %collective-permute-start.18 = (bf16[1024,1024]{1,0:T(8,128)(2,1)S(1)}, bf16[1024,1024]{1,0:T(8,128)(2,1)}, u32[]{:S(2)}, u32[]{:S(2)}) collective-permute-start(bf16[1024,1024]{1,0:T(8,128)(2,1)S(1)} %copy-done.3), channel_id=1, source_target_pairs={{0,6},{32,56},{2,0},{34,58},{4,2},{36,60},{6,4},{38,62},{8,14},{40... | collective-permute-start | bytes 6291464 | tf_op jit(solution)/shard_map/ppermute | solution.py:54
  83.5 16.1 %collective-permute-done.10 = bf16[128,4096]{1,0:T(8,128)(2,1)S(1)} collective-permute-done((bf16[128,4096]{1,0:T(8,128)(2,1)}, bf16[128,4096]{1,0:T(8,128)(2,1)S(1)}, u32[]{:S(2)}, u32[]{:S(2)}) %collective-permute-start.10) | collective-permute-done | bytes 1048608 | tf_op jit(solution)/shard_map/ppermute | solution.py:99
  99.6 1.0 broadcast_select_fusion.1.halo_ref
  100.7 12.0 %forward_conv.1 = (f32[256,4096]{1,0:T(8,128)}, bf16[256,4096]{1,0:T(8,128)(2,1)}) custom-call(f32[256,256]{1,0:T(8,128)} %pad.8.base_ref, f32[1,4096]{1,0:T(1,128)} %bitcast.42, bf16[256,4096]{1,0:T(8,128)(2,1)} %bitcast.32, bf16[256,4096]{1,0:T(8,128)(2,1)} %bitcast.26, bf16[256,4096]{1,0:T(8,128)(2,1)} %bitcast.29, ...), custom_call_target="tpu_custom_call" | custom-call | flops 4294967296 | bytes 14680064 | tf_op jit(solution)/shard_map/forward_conv/pallas_call | solution.py:147
  112.7 0.8 collective-permute-start.12
  114.1 12.4 %collective-permute-done.18.refs_12_ = bf16[1024,1024]{1,0:T(8,128)(2,1)} collective-permute-done((bf16[1024,1024]{1,0:T(8,128)(2,1)S(1)}, bf16[1024,1024]{1,0:T(8,128)(2,1)}, u32[]{:S(2)}, u32[]{:S(2)}) %collective-permute-start.18) | collective-permute-done | bytes 2097184 | tf_op jit(solution)/shard_map/ppermute | solution.py:54
  126.6 3.1 %collective-permute-done.14.refs_8_ = bf16[1024,1024]{1,0:T(8,128)(2,1)} collective-permute-done((bf16[1024,1024]{1,0:T(8,128)(2,1)S(1)}, bf16[1024,1024]{1,0:T(8,128)(2,1)}, u32[]{:S(2)}, u32[]{:S(2)}) %collective-permute-start.14) | collective-permute-done | bytes 2097184 | tf_op jit(solution)/shard_map/ppermute | solution.py:54
  130.3 2.1 collective-permute-start.22
  132.4 1.3 copy-done.13
  134.7 5.7 %adapter_terms.1 = bf16[128,32,128]{2,1,0:T(8,128)(2,1)} custom-call(bf16[256,4096]{1,0:T(8,128)(2,1)} %get-tuple-element.38.signal_ref.refs_1_, bf16[256,4096]{1,0:T(8,128)(2,1)} %bitcast.34, bf16[128,32,128]{2,1,0:T(8,128)(2,1)} %all-to-all-done.shares_ref), custom_call_target="tpu_custom_call" | custom-call | flops 4294967296 | bytes 6291456 | tf_op jit(solution)/shard_map/adapter_terms/pallas_call | solution.py:421
  140.5 26.6 %project.2 = (f32[256,4096]{1,0:T(8,128)}, f32[256,4096]{1,0:T(8,128)}) custom-call(s32[4]{0:T(128)} %pad_add_fusion.refs_0_, bf16[256,4096]{1,0:T(8,128)(2,1)} %get-tuple-element.38.signal_ref.refs_1_, bf16[256,4096]{1,0:T(8,128)(2,1)} %bitcast.35, bf16[1024,1024]{1,0:T(8,128)(2,1)} %constant_dynamic-update-slice_fusion.5.refs_3_, ...), custom_call_target="tpu_custom_call" | custom-call | flops 12884901888 | bytes 41943040 | tf_op jit(solution)/shard_map/project/pallas_call | solution.py:369
  167.7 7.6 %all-to-all-start.1 = ((bf16[128,32,128]{2,1,0:T(8,128)(2,1)}), bf16[128,32,128]{2,1,0:T(8,128)(2,1)S(1)}, u32[]{:S(2)}, u32[]{:S(2)}) async-start(bf16[128,32,128]{2,1,0:T(8,128)(2,1)} %adapter_terms.1), calls=%async_computation.1 | async-start | bytes 2097152 | tf_op jit(solution)/shard_map/all_to_all | solution.py:483
  175.3 16.8 %project.3 = (bf16[256,4096]{1,0:T(8,128)(2,1)}, bf16[256,4096]{1,0:T(8,128)(2,1)}, bf16[128,2048]{1,0:T(8,128)(2,1)}, bf16[128,2048]{1,0:T(8,128)(2,1)}, bf16[128,4096]{1,0:T(8,128)(2,1)}) custom-call(s32[4]{0:T(128)} %pad_add_fusion.refs_0_, bf16[256,4096]{1,0:T(8,128)(2,1)} %get-tuple-element.38.signal_ref.refs_1_, bf16[256,4096]{1,0:T(8,128)(2,1)} %bitcast.36, ...), custom_call_target="tpu_custom_call" | custom-call | flops 4294967296 | bytes 25165824 | tf_op jit(solution)/shard_map/project/pallas_call | solution.py:369
  192.2 2.5 %all-to-all-done.1 = bf16[128,32,128]{2,1,0:T(8,128)(2,1)S(1)} async-done(((bf16[128,32,128]{2,1,0:T(8,128)(2,1)}), bf16[128,32,128]{2,1,0:T(8,128)(2,1)S(1)}, u32[]{:S(2)}, u32[]{:S(2)}) %all-to-all-start.1) | async-done | bytes 1048608 | tf_op jit(solution)/shard_map/all_to_all | solution.py:483
  194.9 1.3 collective-permute-start.26
  196.2 1.3 collective-permute-start.25
  198.2 8.6 %all-to-all-start.2 = ((bf16[32,16,128]{2,1,0:T(8,128)(2,1)}), bf16[32,16,128]{2,1,0:T(8,128)(2,1)S(1)}, u32[]{:S(2)}, u32[]{:S(2)}) async-start(bf16[32,16,128]{2,1,0:T(8,128)(2,1)} %broadcast_in_dim.108), calls=%async_computation.2 | async-start | bytes 262144 | tf_op jit(solution)/shard_map/all_to_all | solution.py:434
  207.5 7.7 %all_gather.3 = bf16[64,128]{1,0:T(8,128)(2,1)S(1)} all-gather(bf16[16,128]{1,0:T(8,128)(2,1)S(1)} %get-tuple-element.73), channel_id=1, replica_groups=mesh['fsdp'=4,'ctx'=32] {'fsdp'}, dimensions={0}, use_global_device_ids=true | all-gather | bytes 20480 | tf_op jit(solution)/shard_map/all_gather | solution.py:433
  215.2 10.1 %all-to-all-done.2 = bf16[32,16,128]{2,1,0:T(8,128)(2,1)S(1)} async-done(((bf16[32,16,128]{2,1,0:T(8,128)(2,1)}), bf16[32,16,128]{2,1,0:T(8,128)(2,1)S(1)}, u32[]{:S(2)}, u32[]{:S(2)}) %all-to-all-start.2) | async-done | bytes 131104 | tf_op jit(solution)/shard_map/all_to_all | solution.py:434
  225.3 0.8 copy-done.15
  226.1 6.7 %backward_conv.2 = (bf16[256,4096]{1,0:T(8,128)(2,1)}, bf16[256,4096]{1,0:T(8,128)(2,1)}) custom-call(f32[256,256]{1,0:T(8,128)} %pad.9.base_ref, f32[1,4096]{1,0:T(1,128)} %bitcast.43, bf16[128,2048]{1,0:T(8,128)(2,1)} %get-tuple-element.54.head_ref, bf16[128,4096]{1,0:T(8,128)(2,1)} %get-tuple-element.53.tail_ref, bf16[128,2048]{1,0:T(8,128)(2,1)} %copy-done.15, ...), custom_call_target="tpu_custom_call" | custom-call | flops 2147483648 | bytes 6291456 | tf_op jit(solution)/shard_map/backward_conv/pallas_call | solution.py:192
  233.6 6.7 %backward_conv.3 = (bf16[256,4096]{1,0:T(8,128)(2,1)}, bf16[256,4096]{1,0:T(8,128)(2,1)}) custom-call(f32[256,256]{1,0:T(8,128)} %pad.9.base_ref, f32[1,4096]{1,0:T(1,128)} %bitcast.44, bf16[128,2048]{1,0:T(8,128)(2,1)} %get-tuple-element.52.head_ref, bf16[128,4096]{1,0:T(8,128)(2,1)} %get-tuple-element.53.tail_ref, ...), custom_call_target="tpu_custom_call", output_to_operand_aliasing={{0}: (7, {}), {1}: (8, {})} | custom-call | flops 2147483648 | bytes 6291456 | tf_op jit(solution)/shard_map/backward_conv/pallas_call | solution.py:192
  (83 shorter events, 10.0 us)
Async XLA Ops:
  0.6 3.8 %copy-start = (bf16[128,64]{0,1:T(8,128)(2,1)S(1)}, bf16[128,64]{0,1:T(8,128)(2,1)}, u32[]{:S(2)}) copy-start(bf16[128,64]{0,1:T(8,128)(2,1)} %param.20) | copy-start | bytes 49156
  0.6 3.6 %copy-start.6 = (s32[128,16]{0,1:T(8,128)S(1)}, s32[128,16]{0,1:T(8,128)}, u32[]{:S(2)}) copy-start(s32[128,16]{0,1:T(8,128)} %param.16) | copy-start | bytes 24580
  0.7 3.6 %copy-start.7 = (f32[128]{0:T(128)S(1)}, f32[128]{0:T(128)}, u32[]{:S(2)}) copy-start(f32[128]{0:T(128)} %param.17) | copy-start | bytes 1540
  0.7 3.8 %copy-start.8 = (bf16[64,1024]{1,0:T(8,128)(2,1)S(1)}, bf16[64,1024]{1,0:T(8,128)(2,1)}, u32[]{:S(2)}) copy-start(bf16[64,1024]{1,0:T(8,128)(2,1)} %param.21) | copy-start | bytes 393220
  2.5 25.3 %collective-permute-start.8 = (bf16[128,4096]{1,0:T(8,128)(2,1)S(1)}, bf16[128,4096]{1,0:T(8,128)(2,1)}, u32[]{:S(2)}, u32[]{:S(2)}) collective-permute-start(bf16[128,4096]{1,0:T(8,128)(2,1)S(1)} %fusion.2), channel_id=1, source_target_pairs={{7,15},{15,23},{23,31},{39,47},{47,55},{55,63},{71,79},{79,87},{87... | collective-permute-start | bytes 3145736 | tf_op jit(solution)/shard_map/ppermute | solution.py:89
  7.0 8.6 %collective-permute-start = (bf16[128,1024]{1,0:T(8,128)(2,1)S(1)}, bf16[128,1024]{1,0:T(8,128)(2,1)S(1)}, u32[]{:S(2)}, u32[]{:S(2)}) collective-permute-start(bf16[128,1024]{1,0:T(8,128)(2,1)S(1)} %get-tuple-element.74), channel_id=1, source_target_pairs={{0,1},{32,34},{2,3},{34,36},{4,5},{36,38},{6,7},{38,32},{8,9},{40,... | collective-permute-start | bytes 786440 | tf_op jit(solution)/shard_map/ppermute | solution.py:54
  9.4 6.2 %collective-permute-start.1 = (bf16[128,1024]{1,0:T(8,128)(2,1)S(1)}, bf16[128,1024]{1,0:T(8,128)(2,1)S(1)}, u32[]{:S(2)}, u32[]{:S(2)}) collective-permute-start(bf16[128,1024]{1,0:T(8,128)(2,1)S(1)} %get-tuple-element.74), channel_id=1, source_target_pairs={{0,65},{32,38},{2,67},{34,32},{4,69},{36,34},{6,71},{38,36},{8,73}... | collective-permute-start | bytes 786440 | tf_op jit(solution)/shard_map/ppermute | solution.py:54
  15.6 5.4 %collective-permute-start.2 = (bf16[64,1024]{1,0:T(8,128)(2,1)S(1)}, bf16[64,1024]{1,0:T(8,128)(2,1)S(1)}, u32[]{:S(2)}, u32[]{:S(2)}) collective-permute-start(bf16[64,1024]{1,0:T(8,128)(2,1)S(1)} %slice.42), channel_id=1, source_target_pairs={{0,1},{32,34},{2,3},{34,36},{4,5},{36,38},{6,7},{38,32},{8,9},{40,... | collective-permute-start | bytes 393224 | tf_op jit(solution)/shard_map/ppermute | solution.py:54
  15.7 6.0 %collective-permute-start.3 = (bf16[64,1024]{1,0:T(8,128)(2,1)S(1)}, bf16[64,1024]{1,0:T(8,128)(2,1)S(1)}, u32[]{:S(2)}, u32[]{:S(2)}) collective-permute-start(bf16[64,1024]{1,0:T(8,128)(2,1)S(1)} %slice.43), channel_id=1, source_target_pairs={{0,65},{32,38},{2,67},{34,32},{4,69},{36,34},{6,71},{38,36},{8,73}... | collective-permute-start | bytes 393224 | tf_op jit(solution)/shard_map/ppermute | solution.py:54
  22.4 1.0 copy-start.14
  23.3 24.6 %collective-permute-start.5 = (bf16[512,1024]{1,0:T(8,128)(2,1)}, bf16[512,1024]{1,0:T(8,128)(2,1)S(1)}, u32[]{:S(2)}, u32[]{:S(2)}) collective-permute-start(bf16[512,1024]{1,0:T(8,128)(2,1)} %copy-done.14), channel_id=1, source_target_pairs={{0,8},{32,33},{2,10},{34,35},{4,12},{36,37},{6,14},{38,39},{8,16},... | collective-permute-start | bytes 3145736 | tf_op jit(solution)/shard_map/ppermute | solution.py:54
  26.5 23.6 %collective-permute-start.4 = (bf16[512,1024]{1,0:T(8,128)(2,1)}, bf16[512,1024]{1,0:T(8,128)(2,1)S(1)}, u32[]{:S(2)}, u32[]{:S(2)}) collective-permute-start(bf16[512,1024]{1,0:T(8,128)(2,1)} %copy-done.14), channel_id=1, source_target_pairs={{0,24},{32,97},{2,26},{34,99},{4,28},{36,101},{6,30},{38,103},{8,0... | collective-permute-start | bytes 3145736 | tf_op jit(solution)/shard_map/ppermute | solution.py:54
  28.9 41.4 %collective-permute-start.9 = (bf16[128,4096]{1,0:T(8,128)(2,1)}, bf16[128,4096]{1,0:T(8,128)(2,1)}, u32[]{:S(2)}, u32[]{:S(2)}) collective-permute-start(bf16[128,4096]{1,0:T(8,128)(2,1)} %broadcast_select_fusion.2), channel_id=1, source_target_pairs={{1,3},{3,5},{5,7},{9,11},{11,13},{13,15},{15,9},{17,19},{19,21},{2... | collective-permute-start | bytes 3145736 | tf_op jit(solution)/shard_map/ppermute | solution.py:94
  31.7 38.6 %all-to-all-start = ((bf16[128,32,128]{2,1,0:T(8,128)(2,1)}), bf16[128,32,128]{2,1,0:T(8,128)(2,1)}, u32[]{:S(2)}, u32[]{:S(2)}) async-start(bf16[128,32,128]{2,1,0:T(8,128)(2,1)} %broadcast_in_dim.102), calls=%async_computation | async-start | bytes 2097152 | tf_op jit(solution)/shard_map/all_to_all | solution.py:387
  48.8 18.8 %collective-permute-start.6 = (bf16[256,1024]{1,0:T(8,128)(2,1)}, bf16[256,1024]{1,0:T(8,128)(2,1)}, u32[]{:S(2)}, u32[]{:S(2)}) collective-permute-start(bf16[256,1024]{1,0:T(8,128)(2,1)} %slice.44), channel_id=1, source_target_pairs={{0,8},{32,33},{2,10},{34,35},{4,12},{36,37},{6,14},{38,39},{8,16},... | collective-permute-start | bytes 1572872 | tf_op jit(solution)/shard_map/ppermute | solution.py:54
  51.0 16.6 %collective-permute-start.7 = (bf16[256,1024]{1,0:T(8,128)(2,1)}, bf16[256,1024]{1,0:T(8,128)(2,1)}, u32[]{:S(2)}, u32[]{:S(2)}) collective-permute-start(bf16[256,1024]{1,0:T(8,128)(2,1)} %slice.45), channel_id=1, source_target_pairs={{0,24},{32,97},{2,26},{34,99},{4,28},{36,101},{6,30},{38,103},{8,0... | collective-permute-start | bytes 1572872 | tf_op jit(solution)/shard_map/ppermute | solution.py:54
  70.3 5.8 %copy-start.5 = (bf16[256,128]{1,0:T(8,128)(2,1)S(1)}, bf16[256,128]{1,0:T(8,128)(2,1)}, u32[]{:S(2)}) copy-start(bf16[256,128]{1,0:T(8,128)(2,1)} %param.18) | copy-start | bytes 196612
  70.3 10.6 %copy-start.3 = (bf16[1024,1024]{1,0:T(8,128)(2,1)S(1)}, bf16[1024,1024]{1,0:T(8,128)(2,1)}, u32[]{:S(2)}) copy-start(bf16[1024,1024]{1,0:T(8,128)(2,1)} %pad_maximum_fusion.refs_4_) | copy-start | bytes 6291460
  71.4 28.2 %collective-permute-start.10 = (bf16[128,4096]{1,0:T(8,128)(2,1)}, bf16[128,4096]{1,0:T(8,128)(2,1)S(1)}, u32[]{:S(2)}, u32[]{:S(2)}) collective-permute-start(bf16[128,4096]{1,0:T(8,128)(2,1)} %broadcast_select_fusion), channel_id=1, source_target_pairs={{0,1},{1,0},{2,3},{3,2},{4,5},{5,4},{6,7},{7,6},{8,9},{9,8},{10,11... | collective-permute-start | bytes 3145736 | tf_op jit(solution)/shard_map/ppermute | solution.py:99
  77.1 36.4 %collective-permute-start.17 = (bf16[1024,1024]{1,0:T(8,128)(2,1)}, bf16[1024,1024]{1,0:T(8,128)(2,1)S(1)}, u32[]{:S(2)}, u32[]{:S(2)}) collective-permute-start(bf16[1024,1024]{1,0:T(8,128)(2,1)} %constant_dynamic-update-slice_fusion.5.refs_3_), channel_id=1, source_target_pairs={{0,6},{32,56},{2,0},{34,58},{4,2},{36,60},{6,4},{38,62},{8,14},{40... | collective-permute-start | bytes 6291464 | tf_op jit(solution)/shard_map/ppermute | solution.py:54
  80.8 32.8 %collective-permute-start.13 = (bf16[1024,1024]{1,0:T(8,128)(2,1)}, bf16[1024,1024]{1,0:T(8,128)(2,1)}, u32[]{:S(2)}, u32[]{:S(2)}) collective-permute-start(bf16[1024,1024]{1,0:T(8,128)(2,1)} %constant_dynamic-update-slice_fusion.5.refs_3_), channel_id=1, source_target_pairs={{0,2},{32,40},{2,4},{34,42},{4,6},{36,44},{6,0},{38,46},{8,10},{40... | collective-permute-start | bytes 6291464 | tf_op jit(solution)/shard_map/ppermute | solution.py:54
  80.9 45.7 %collective-permute-start.18 = (bf16[1024,1024]{1,0:T(8,128)(2,1)S(1)}, bf16[1024,1024]{1,0:T(8,128)(2,1)}, u32[]{:S(2)}, u32[]{:S(2)}) collective-permute-start(bf16[1024,1024]{1,0:T(8,128)(2,1)S(1)} %copy-done.3), channel_id=1, source_target_pairs={{0,6},{32,56},{2,0},{34,58},{4,2},{36,60},{6,4},{38,62},{8,14},{40... | collective-permute-start | bytes 6291464 | tf_op jit(solution)/shard_map/ppermute | solution.py:54
  83.5 46.2 %collective-permute-start.14 = (bf16[1024,1024]{1,0:T(8,128)(2,1)S(1)}, bf16[1024,1024]{1,0:T(8,128)(2,1)}, u32[]{:S(2)}, u32[]{:S(2)}) collective-permute-start(bf16[1024,1024]{1,0:T(8,128)(2,1)S(1)} %copy-done.3), channel_id=1, source_target_pairs={{0,2},{32,40},{2,4},{34,42},{4,6},{36,44},{6,0},{38,46},{8,10},{40... | collective-permute-start | bytes 6291464 | tf_op jit(solution)/shard_map/ppermute | solution.py:54
  100.7 12.8 %copy-start.10 = (bf16[1024,1024]{1,0:T(8,128)(2,1)S(1)}, bf16[1024,1024]{1,0:T(8,128)(2,1)}, u32[]{:S(2)}) copy-start(bf16[1024,1024]{1,0:T(8,128)(2,1)} %constant_dynamic-update-slice_fusion.5.refs_3_) | copy-start | bytes 6291460
  112.7 17.1 %collective-permute-start.12 = (bf16[1024,1024]{1,0:T(8,128)(2,1)S(1)}, bf16[1024,1024]{1,0:T(8,128)(2,1)S(1)}, u32[]{:S(2)}, u32[]{:S(2)}) collective-permute-start(bf16[1024,1024]{1,0:T(8,128)(2,1)S(1)} %copy-done.3), channel_id=1, source_target_pairs={{0,32},{32,0},{2,34},{34,2},{4,36},{36,4},{6,38},{38,6},{8,40},{40... | collective-permute-start | bytes 6291464 | tf_op jit(solution)/shard_map/ppermute | solution.py:65
  113.5 16.8 %copy-start.9 = (bf16[1024,1024]{1,0:T(8,128)(2,1)}, bf16[1024,1024]{1,0:T(8,128)(2,1)S(1)}, u32[]{:S(2)}) copy-start(bf16[1024,1024]{1,0:T(8,128)(2,1)S(1)} %collective-permute-done.17.refs_11_) | copy-start | bytes 6291460
  113.5 16.8 %collective-permute-start.11 = (bf16[1024,1024]{1,0:T(8,128)(2,1)S(1)}, bf16[1024,1024]{1,0:T(8,128)(2,1)S(1)}, u32[]{:S(2)}, u32[]{:S(2)}) collective-permute-start(bf16[1024,1024]{1,0:T(8,128)(2,1)S(1)} %copy-done.10), channel_id=1, source_target_pairs={{0,32},{32,0},{2,34},{34,2},{4,36},{36,4},{6,38},{38,6},{8,40},{40... | collective-permute-start | bytes 6291464 | tf_op jit(solution)/shard_map/ppermute | solution.py:65
  113.6 18.8 %collective-permute-start.19 = (bf16[1024,1024]{1,0:T(8,128)(2,1)S(1)}, bf16[1024,1024]{1,0:T(8,128)(2,1)S(1)}, u32[]{:S(2)}, u32[]{:S(2)}) collective-permute-start(bf16[1024,1024]{1,0:T(8,128)(2,1)S(1)} %collective-permute-done.17.refs_11_), channel_id=1, source_target_pairs={{0,32},{32,0},{2,34},{34,2},{4,36},{36,4},{6,38},{38,6},{8,40},{40... | collective-permute-start | bytes 6291464 | tf_op jit(solution)/shard_map/ppermute | solution.py:65
  126.5 14.0 %collective-permute-start.15 = (bf16[1024,1024]{1,0:T(8,128)(2,1)}, bf16[1024,1024]{1,0:T(8,128)(2,1)}, u32[]{:S(2)}, u32[]{:S(2)}) collective-permute-start(bf16[1024,1024]{1,0:T(8,128)(2,1)} %collective-permute-done.13.refs_7_), channel_id=1, source_target_pairs={{0,32},{32,0},{2,34},{34,2},{4,36},{36,4},{6,38},{38,6},{8,40},{40... | collective-permute-start | bytes 6291464 | tf_op jit(solution)/shard_map/ppermute | solution.py:65
  129.7 10.7 %collective-permute-start.20 = (bf16[1024,1024]{1,0:T(8,128)(2,1)}, bf16[1024,1024]{1,0:T(8,128)(2,1)}, u32[]{:S(2)}, u32[]{:S(2)}) collective-permute-start(bf16[1024,1024]{1,0:T(8,128)(2,1)} %collective-permute-done.18.refs_12_), channel_id=1, source_target_pairs={{0,32},{32,0},{2,34},{34,2},{4,36},{36,4},{6,38},{38,6},{8,40},{40... | collective-permute-start | bytes 6291464 | tf_op jit(solution)/shard_map/ppermute | solution.py:65
  129.7 2.6 %copy-start.11 = (bf16[1024,1024]{1,0:T(8,128)(2,1)}, bf16[1024,1024]{1,0:T(8,128)(2,1)S(1)}, u32[]{:S(2)}) copy-start(bf16[1024,1024]{1,0:T(8,128)(2,1)S(1)} %collective-permute-done.12.refs_6_) | copy-start | bytes 6291460
  129.7 10.7 %collective-permute-start.16 = (bf16[1024,1024]{1,0:T(8,128)(2,1)}, bf16[1024,1024]{1,0:T(8,128)(2,1)}, u32[]{:S(2)}, u32[]{:S(2)}) collective-permute-start(bf16[1024,1024]{1,0:T(8,128)(2,1)} %collective-permute-done.14.refs_8_), channel_id=1, source_target_pairs={{0,32},{32,0},{2,34},{34,2},{4,36},{36,4},{6,38},{38,6},{8,40},{40... | collective-permute-start | bytes 6291464 | tf_op jit(solution)/shard_map/ppermute | solution.py:65
  130.3 2.1 copy-start.12
  130.3 36.8 %collective-permute-start.22 = (bf16[1024,1024]{1,0:T(8,128)(2,1)}, bf16[1024,1024]{1,0:T(8,128)(2,1)S(1)}, u32[]{:S(2)}, u32[]{:S(2)}) collective-permute-start(bf16[1024,1024]{1,0:T(8,128)(2,1)} %collective-permute-done.18.refs_12_), channel_id=1, source_target_pairs={{0,6},{32,56},{2,0},{34,58},{4,2},{36,60},{6,4},{38,62},{8,14},{40... | collective-permute-start | bytes 6291464 | tf_op jit(solution)/shard_map/ppermute | solution.py:54
  132.4 1.3 copy-start.13
  133.7 33.5 %collective-permute-start.21 = (bf16[1024,1024]{1,0:T(8,128)(2,1)}, bf16[1024,1024]{1,0:T(8,128)(2,1)}, u32[]{:S(2)}, u32[]{:S(2)}) collective-permute-start(bf16[1024,1024]{1,0:T(8,128)(2,1)} %collective-permute-done.13.refs_7_), channel_id=1, source_target_pairs={{0,2},{32,40},{2,4},{34,42},{4,6},{36,44},{6,0},{38,46},{8,10},{40... | collective-permute-start | bytes 6291464 | tf_op jit(solution)/shard_map/ppermute | solution.py:54
  167.1 8.2 %copy-start.2 = (bf16[1024,1024]{1,0:T(8,128)(2,1)}, bf16[1024,1024]{1,0:T(8,128)(2,1)S(1)}, u32[]{:S(2)}) copy-start(bf16[1024,1024]{1,0:T(8,128)(2,1)S(1)} %collective-permute-done.22.refs_6_) | copy-start | bytes 6291460
  167.1 8.2 %collective-permute-start.24 = (bf16[1024,1024]{1,0:T(8,128)(2,1)S(1)}, bf16[1024,1024]{1,0:T(8,128)(2,1)}, u32[]{:S(2)}, u32[]{:S(2)}) collective-permute-start(bf16[1024,1024]{1,0:T(8,128)(2,1)S(1)} %collective-permute-done.22.refs_6_), channel_id=1, source_target_pairs={{0,32},{32,0},{2,34},{34,2},{4,36},{36,4},{6,38},{38,6},{8,40},{40... | collective-permute-start | bytes 6291464 | tf_op jit(solution)/shard_map/ppermute | solution.py:65
  167.2 8.1 %collective-permute-start.23 = (bf16[1024,1024]{1,0:T(8,128)(2,1)}, bf16[1024,1024]{1,0:T(8,128)(2,1)}, u32[]{:S(2)}, u32[]{:S(2)}) collective-permute-start(bf16[1024,1024]{1,0:T(8,128)(2,1)} %collective-permute-done.21.refs_5_), channel_id=1, source_target_pairs={{0,32},{32,0},{2,34},{34,2},{4,36},{36,4},{6,38},{38,6},{8,40},{40... | collective-permute-start | bytes 6291464 | tf_op jit(solution)/shard_map/ppermute | solution.py:65
  167.7 27.0 %all-to-all-start.1 = ((bf16[128,32,128]{2,1,0:T(8,128)(2,1)}), bf16[128,32,128]{2,1,0:T(8,128)(2,1)S(1)}, u32[]{:S(2)}, u32[]{:S(2)}) async-start(bf16[128,32,128]{2,1,0:T(8,128)(2,1)} %adapter_terms.1), calls=%async_computation.1 | async-start | bytes 2097152 | tf_op jit(solution)/shard_map/all_to_all | solution.py:483
  194.9 30.4 %collective-permute-start.26 = (bf16[128,2048]{1,0:T(8,128)(2,1)}, bf16[128,2048]{1,0:T(8,128)(2,1)S(1)}, u32[]{:S(2)}, u32[]{:S(2)}) collective-permute-start(bf16[128,2048]{1,0:T(8,128)(2,1)} %get-tuple-element.54.head_ref), channel_id=1, source_target_pairs={{1,0},{2,1},{3,2},{4,3},{5,4},{6,5},{7,6},{8,7},{9,8},{10,9},{11,1... | collective-permute-start | bytes 1572872 | tf_op jit(solution)/shard_map/ppermute | solution.py:83
  196.2 36.6 %collective-permute-start.25 = (bf16[128,2048]{1,0:T(8,128)(2,1)}, bf16[128,2048]{1,0:T(8,128)(2,1)S(1)}, u32[]{:S(2)}, u32[]{:S(2)}) collective-permute-start(bf16[128,2048]{1,0:T(8,128)(2,1)} %get-tuple-element.52.head_ref), channel_id=1, source_target_pairs={{1,0},{2,1},{3,2},{4,3},{5,4},{6,5},{7,6},{8,7},{9,8},{10,9},{11,1... | collective-permute-start | bytes 1572872 | tf_op jit(solution)/shard_map/ppermute | solution.py:83
  198.2 27.1 %all-to-all-start.2 = ((bf16[32,16,128]{2,1,0:T(8,128)(2,1)}), bf16[32,16,128]{2,1,0:T(8,128)(2,1)S(1)}, u32[]{:S(2)}, u32[]{:S(2)}) async-start(bf16[32,16,128]{2,1,0:T(8,128)(2,1)} %broadcast_in_dim.108), calls=%async_computation.2 | async-start | bytes 262144 | tf_op jit(solution)/shard_map/all_to_all | solution.py:434
  225.3 0.8 copy-start.15
  232.8 0.8 copy-start.4
  233.6 8.0 %copy-start.1 = (bf16[128,64]{0,1:T(8,128)(2,1)S(1)}, bf16[128,64]{0,1:T(8,128)(2,1)}, u32[]{:S(2)}) copy-start(bf16[128,64]{0,1:T(8,128)(2,1)} %param.20) | copy-start | bytes 49156

commit v3 on v2

--- a/solution.py
+++ b/solution.py
@@ -428,12 +428,23 @@
     )(signal, cot, shares)
 
 
-def adapter_results(parts, multiplier):
+def adapter_sums(parts, multiplier):
     sums = (multiplier * jnp.sum(parts.astype(jnp.float32), 0)).astype(jnp.bfloat16)
-    grad_down = lax.all_gather(sums[:16], "fsdp", axis=0, tiled=True)
+    mine = sums[:16]
+    others = [lax.ppermute(mine, "fsdp", [(i, i ^ k) for i in range(4)]) for k in (1, 2, 3)]
     up = lax.all_to_all(jnp.broadcast_to(sums[None, 16:], (32, 16, 128)), "ctx", 0, 0, tiled=True)
-    grad_up = jnp.transpose(up.reshape(8, 4, 2, 8, 128), (0, 3, 1, 2, 4)).reshape(64, 1024)
-    return grad_down.T, grad_up
+    return [mine] + others, up
+
+
+def adapter_down(blocks, fsdp):
+    odd, high = fsdp % 2 == 1, fsdp // 2 == 1
+    blocks = [jnp.where(odd, blocks[k ^ 1], blocks[k]) for k in range(4)]
+    blocks = [jnp.where(high, blocks[k ^ 2], blocks[k]) for k in range(4)]
+    return jnp.concatenate(blocks, 0).T
+
+
+def adapter_up(up):
+    return jnp.transpose(up.reshape(8, 4, 2, 8, 128), (0, 3, 1, 2, 4)).reshape(64, 1024)
 
 
 def local(
@@ -479,11 +490,11 @@
 
     far_front = send(after(plus_front, signal), 2, 1, 1)
     far_rear = send(minus_rear, 2, 1, -1)
-    terms = adapter_terms(signal, cot, shares)
+    terms = adapter_terms(after(signal, plus_front), cot, shares)
     parts = lax.all_to_all(terms, BOTH, 0, 0, tiled=True)
-    swapped = [
-        swap_cores(after(block, signal))
-        for block in (front, rear, plus_front, plus_rear, minus_front, minus_rear)
+    swapped = [swap_cores(after(block, signal)) for block in (front, rear)]
+    swapped += [
+        swap_cores(after(block, terms)) for block in (plus_front, plus_rear, minus_front, minus_rear)
     ]
     sums = project(
         meta,
@@ -509,11 +520,13 @@
         (gated, query),
     )
     halo_a, halo_b = along_ctx(head_a, -1), along_ctx(head_b, -1)
-    grad_down, grad_up = adapter_results(after(parts, output), multiplier)
+    down_blocks, up_blocks = adapter_sums(after(parts, output), multiplier)
     results = backward_conv(backward_base, skip, head_a, tail, halo_a, key, value, 0, ())
     grad_key, grad_value = backward_conv(
         backward_base, skip, head_b, tail, halo_b, key, value, 1, tuple(results)
     )
+    grad_up = adapter_up(after(up_blocks, grad_key))
+    grad_down = adapter_down(after(down_blocks, grad_key), fsdp)
     return output[None], grad_query[None], grad_key[None], grad_value[None], grad_down, grad_up
 
 

time: 245 us -> 233 us (0.951)
  waiting for transfers between devices: 63.6 us -> 51.5 us
  blocking collectives: 7.67 us -> 0 us
  starting transfers between devices: 69.1 us -> 76.7 us
    all_to_all x1, waiting for transfers between devices: 10.1 us -> 0.01 us  [adapter_sums(): lax.all_to_all(jnp.broadcast_to(sums[None, 16:], (32, 16, 128)), 'ctx', 0...]
    ppermute x14, waiting for transfers between devices: 34.9 us -> 27 us  [send(): return lax.ppermute(block, BOTH, ring_pairs(axis0, axis1, step))]
    all_gather x1 -> x0, blocking collectives: 7.67 us -> none  [adapter_results(): grad_down = lax.all_gather(sums[:16], 'fsdp', axis=0, tiled=True)]
    ppermute x0 -> x3, starting transfers between devices: none -> 4.38 us  [adapter_sums(): lax.ppermute(mine, 'fsdp', [(i, i ^ k) for i in range(4)])]
    ppermute x8, waiting for transfers between devices: 0.02 us -> 4.33 us  [swap_cores(): return lax.ppermute(block, BOTH, pairs)]
    all_to_all x1, starting transfers between devices: 7.61 us -> 10.3 us  [local(): parts = lax.all_to_all(terms, BOTH, 0, 0, tiled=True)]
    unnamed x38 -> x35, local copies, waits for them, and re-layouts: 8.06 us -> 7.47 us
  transfers between devices with their start and end apart: 30 -> 33, of which waited for: 8 -> 9; matrix products, arithmetic and copies ran while one was open for 7% -> 8% of each run, Pallas kernels for 28% -> 33%
where the time goes in v3:
time: 233 us; the launch traced here: 229 us
  starting transfers between devices  76.7 us (33%)
  Pallas kernels  74.6 us (32%)
  waiting for transfers between devices  51.5 us (22%)
  local copies, waits for them, and re-layouts  14 us (6%)
  other arithmetic  9.17 us (4%)
  matrix products  2.48 us (1%)
    pallas_call x2, Pallas kernels, project(): pl.pallas_call(functools.partial(project_kernel, groups=static, first=fir...  43.4 us
    ppermute x14, waiting for transfers between devices, send(): return lax.ppermute(block, BOTH, ring_pairs(axis0, axis1, step))  27 us
    ppermute x14, starting transfers between devices, send(): return lax.ppermute(block, BOTH, ring_pairs(axis0, axis1, step))  23.4 us
    ppermute x1, waiting for transfers between devices, pair_rows(): lax.ppermute(jnp.where(ctx % 2 == 0, block, relayed), 'ctx', [(i, i ^ 1)...  17.3 us
    all_to_all x1, starting transfers between devices, gathered_adapters(): lax.all_to_all(jnp.broadcast_to(share[None], (128, 32, 128)), BOTH, 0, 0,...  16.2 us
    pallas_call x2, Pallas kernels, backward_conv(): pl.pallas_call(functools.partial(backward_kernel, tiles=width // 128), gr...  13.5 us
    pallas_call x1, Pallas kernels, forward_conv(): pl.pallas_call(functools.partial(forward_kernel, tiles=width // 128), gri...  12 us
    all_to_all x1, starting transfers between devices, local(): parts = lax.all_to_all(terms, BOTH, 0, 0, tiled=True)  10.3 us
  transfers between devices with their start and end apart: 33, of which 9 were waited for; matrix products, arithmetic and copies ran while one was open for 8% of the time, Pallas kernels for 33%

profile of v3, /device:TPU:1, one launch (start us, length us, event | category | flops | bytes accessed | tf_op | source)
XLA Modules:
  0.0 229.4 jit_solution(6412696035990893020)
XLA Ops:
  0.7 1.8 fusion.2
  2.5 1.7 collective-permute-start.8
  4.5 2.5 %constant_dynamic-update-slice_fusion.10 = (bf16[1024,1024]{1,0:T(8,128)(2,1)}, bf16[512,1024]{1,0:T(8,128)(2,1)S(1)}, bf16[128,1024]{1,0:T(8,128)(2,1)S(1)}) fusion(bf16[128,64]{0,1:T(8,128)(2,1)S(1)} %copy-done, bf16[64,1024]{1,0:T(8,128)(2,1)S(1)} %copy-done.8, f32[128,1024]{1,0:T(8,128)S(1)} %copy.20, s32[128,1024]{1,0:T(8,128)} %param.15), kind=kOutput, calls=%fused_computation.21 | convolution fusion | flops 21757952 | bytes 1982464 | tf_op jit(solution)/shard_map/dot_general | solution.py:112
  7.0 2.5 %collective-permute-start = (bf16[128,1024]{1,0:T(8,128)(2,1)S(1)}, bf16[128,1024]{1,0:T(8,128)(2,1)S(1)}, u32[]{:S(2)}, u32[]{:S(2)}) collective-permute-start(bf16[128,1024]{1,0:T(8,128)(2,1)S(1)} %get-tuple-element.92), channel_id=1, source_target_pairs={{0,1},{32,34},{2,3},{34,36},{4,5},{36,38},{6,7},{38,32},{8,9},{40,... | collective-permute-start | bytes 786440 | tf_op jit(solution)/shard_map/ppermute | solution.py:54
  9.4 2.1 collective-permute-start.1
  11.6 4.0 %collective-permute-done = bf16[128,1024]{1,0:T(8,128)(2,1)S(1)} collective-permute-done((bf16[128,1024]{1,0:T(8,128)(2,1)S(1)}, bf16[128,1024]{1,0:T(8,128)(2,1)S(1)}, u32[]{:S(2)}, u32[]{:S(2)}) %collective-permute-start) | collective-permute-done | bytes 262176 | tf_op jit(solution)/shard_map/ppermute | solution.py:54
  15.7 2.7 %collective-permute-start.3 = (bf16[64,1024]{1,0:T(8,128)(2,1)S(1)}, bf16[64,1024]{1,0:T(8,128)(2,1)S(1)}, u32[]{:S(2)}, u32[]{:S(2)}) collective-permute-start(bf16[64,1024]{1,0:T(8,128)(2,1)S(1)} %slice.43), channel_id=1, source_target_pairs={{0,65},{32,38},{2,67},{34,32},{4,69},{36,34},{6,71},{38,36},{8,73}... | collective-permute-start | bytes 393224 | tf_op jit(solution)/shard_map/ppermute | solution.py:54
  19.9 1.0 collective-permute-done.2
  22.3 1.0 copy-done.13
  23.3 3.2 %collective-permute-start.5 = (bf16[512,1024]{1,0:T(8,128)(2,1)}, bf16[512,1024]{1,0:T(8,128)(2,1)S(1)}, u32[]{:S(2)}, u32[]{:S(2)}) collective-permute-start(bf16[512,1024]{1,0:T(8,128)(2,1)} %copy-done.13), channel_id=1, source_target_pairs={{0,8},{32,33},{2,10},{34,35},{4,12},{36,37},{6,14},{38,39},{8,16},... | collective-permute-start | bytes 3145736 | tf_op jit(solution)/shard_map/ppermute | solution.py:54
  26.5 1.3 collective-permute-start.4
  27.8 1.1 broadcast_select_fusion.2
  28.9 1.7 collective-permute-start.9
  30.6 1.1 broadcast_in_dim.102
  31.7 16.2 %all-to-all-start = ((bf16[128,32,128]{2,1,0:T(8,128)(2,1)}), bf16[128,32,128]{2,1,0:T(8,128)(2,1)}, u32[]{:S(2)}, u32[]{:S(2)}) async-start(bf16[128,32,128]{2,1,0:T(8,128)(2,1)} %broadcast_in_dim.102), calls=%async_computation | async-start | bytes 2097152 | tf_op jit(solution)/shard_map/all_to_all | solution.py:387
  47.9 0.8 slice.44
  48.8 1.4 collective-permute-start.6
  51.0 1.3 collective-permute-start.7
  52.3 1.0 constant_dynamic-update-slice_fusion.5.refs_3_
  53.3 14.3 %collective-permute-done.6 = bf16[256,1024]{1,0:T(8,128)(2,1)} collective-permute-done((bf16[256,1024]{1,0:T(8,128)(2,1)}, bf16[256,1024]{1,0:T(8,128)(2,1)}, u32[]{:S(2)}, u32[]{:S(2)}) %collective-permute-start.6) | collective-permute-done | bytes 524320 | tf_op jit(solution)/shard_map/ppermute | solution.py:54
  67.6 2.7 %pad_maximum_fusion.refs_4_ = bf16[1024,1024]{1,0:T(8,128)(2,1)} fusion(bf16[256,1024]{1,0:T(8,128)(2,1)} %collective-permute-done.7, bf16[256,1024]{1,0:T(8,128)(2,1)} %collective-permute-done.6, bf16[512,1024]{1,0:T(8,128)(2,1)S(1)} %collective-permute-done.4), kind=kLoop, calls=%fused_computation | loop fusion | flops 6291456 | bytes 4194304 | tf_op jit(solution)/shard_map/concatenate | solution.py:480
  70.3 1.1 broadcast_select_fusion
  71.4 4.7 %collective-permute-start.10 = (bf16[128,4096]{1,0:T(8,128)(2,1)}, bf16[128,4096]{1,0:T(8,128)(2,1)S(1)}, u32[]{:S(2)}, u32[]{:S(2)}) collective-permute-start(bf16[128,4096]{1,0:T(8,128)(2,1)} %broadcast_select_fusion), channel_id=1, source_target_pairs={{0,1},{1,0},{2,3},{3,2},{4,5},{5,4},{6,7},{7,6},{8,9},{9,8},{10,11... | collective-permute-start | bytes 3145736 | tf_op jit(solution)/shard_map/ppermute | solution.py:99
  76.3 0.9 pad.8.base_ref
  77.1 2.3 %collective-permute-start.11 = (bf16[1024,1024]{1,0:T(8,128)(2,1)}, bf16[1024,1024]{1,0:T(8,128)(2,1)}, u32[]{:S(2)}, u32[]{:S(2)}) collective-permute-start(bf16[1024,1024]{1,0:T(8,128)(2,1)} %constant_dynamic-update-slice_fusion.5.refs_3_), channel_id=1, source_target_pairs={{0,2},{32,40},{2,4},{34,42},{4,6},{36,44},{6,0},{38,46},{8,10},{40... | collective-permute-start | bytes 6291464 | tf_op jit(solution)/shard_map/ppermute | solution.py:54
  79.4 1.4 collective-permute-start.17
  80.9 1.5 collective-permute-start.18
  82.3 17.3 %collective-permute-done.10 = bf16[128,4096]{1,0:T(8,128)(2,1)S(1)} collective-permute-done((bf16[128,4096]{1,0:T(8,128)(2,1)}, bf16[128,4096]{1,0:T(8,128)(2,1)S(1)}, u32[]{:S(2)}, u32[]{:S(2)}) %collective-permute-start.10) | collective-permute-done | bytes 1048608 | tf_op jit(solution)/shard_map/ppermute | solution.py:99
  99.6 1.0 broadcast_select_fusion.1.halo_ref
  100.7 12.0 %forward_conv.1 = (f32[256,4096]{1,0:T(8,128)}, bf16[256,4096]{1,0:T(8,128)(2,1)}) custom-call(f32[256,256]{1,0:T(8,128)} %pad.8.base_ref, f32[1,4096]{1,0:T(1,128)} %bitcast.42, bf16[256,4096]{1,0:T(8,128)(2,1)} %bitcast.33, bf16[256,4096]{1,0:T(8,128)(2,1)} %bitcast.27, bf16[256,4096]{1,0:T(8,128)(2,1)} %bitcast.30, ...), custom_call_target="tpu_custom_call" | custom-call | flops 4294967296 | bytes 14680064 | tf_op jit(solution)/shard_map/forward_conv/pallas_call | solution.py:147
  113.6 5.7 %adapter_terms.1 = bf16[128,32,128]{2,1,0:T(8,128)(2,1)} custom-call(bf16[256,4096]{1,0:T(8,128)(2,1)} %get-tuple-element.46.signal_ref.refs_1_, bf16[256,4096]{1,0:T(8,128)(2,1)} %bitcast.35, bf16[128,32,128]{2,1,0:T(8,128)(2,1)} %all-to-all-done.shares_ref), custom_call_target="tpu_custom_call" | custom-call | flops 4294967296 | bytes 6291456 | tf_op jit(solution)/shard_map/adapter_terms/pallas_call | solution.py:421
  119.8 7.6 %collective-permute-done.18.refs_12_ = bf16[1024,1024]{1,0:T(8,128)(2,1)} collective-permute-done((bf16[1024,1024]{1,0:T(8,128)(2,1)S(1)}, bf16[1024,1024]{1,0:T(8,128)(2,1)}, u32[]{:S(2)}, u32[]{:S(2)}) %collective-permute-start.18) | collective-permute-done | bytes 2097184 | tf_op jit(solution)/shard_map/ppermute | solution.py:54
  128.0 3.7 %collective-permute-start.22 = (bf16[1024,1024]{1,0:T(8,128)(2,1)}, bf16[1024,1024]{1,0:T(8,128)(2,1)S(1)}, u32[]{:S(2)}, u32[]{:S(2)}) collective-permute-start(bf16[1024,1024]{1,0:T(8,128)(2,1)} %collective-permute-done.18.refs_12_), channel_id=1, source_target_pairs={{0,6},{32,56},{2,0},{34,58},{4,2},{36,60},{6,4},{38,62},{8,14},{40... | collective-permute-start | bytes 6291464 | tf_op jit(solution)/shard_map/ppermute | solution.py:54
  131.7 1.3 copy-done.12
  133.6 1.3 collective-permute-done.20.refs_14_
  134.9 3.0 %collective-permute-done.16.refs_10_ = bf16[1024,1024]{1,0:T(8,128)(2,1)} collective-permute-done((bf16[1024,1024]{1,0:T(8,128)(2,1)}, bf16[1024,1024]{1,0:T(8,128)(2,1)}, u32[]{:S(2)}, u32[]{:S(2)}) %collective-permute-start.16) | collective-permute-done | bytes 2097184 | tf_op jit(solution)/shard_map/ppermute | solution.py:65
  137.9 26.6 %project.2 = (f32[256,4096]{1,0:T(8,128)}, f32[256,4096]{1,0:T(8,128)}) custom-call(s32[4]{0:T(128)} %pad_add_fusion.refs_0_, bf16[256,4096]{1,0:T(8,128)(2,1)} %get-tuple-element.46.signal_ref.refs_1_, bf16[256,4096]{1,0:T(8,128)(2,1)} %bitcast.36, bf16[1024,1024]{1,0:T(8,128)(2,1)} %constant_dynamic-update-slice_fusion.5.refs_3_, ...), custom_call_target="tpu_custom_call" | custom-call | flops 12884901888 | bytes 41943040 | tf_op jit(solution)/shard_map/project/pallas_call | solution.py:369
  165.1 10.3 %all-to-all-start.1 = ((bf16[128,32,128]{2,1,0:T(8,128)(2,1)}), bf16[128,32,128]{2,1,0:T(8,128)(2,1)S(1)}, u32[]{:S(2)}, u32[]{:S(2)}) async-start(bf16[128,32,128]{2,1,0:T(8,128)(2,1)} %adapter_terms.1), calls=%async_computation.1 | async-start | bytes 2097152 | tf_op jit(solution)/shard_map/all_to_all | solution.py:494
  176.2 16.8 %project.3 = (bf16[256,4096]{1,0:T(8,128)(2,1)}, bf16[256,4096]{1,0:T(8,128)(2,1)}, bf16[128,2048]{1,0:T(8,128)(2,1)}, bf16[128,2048]{1,0:T(8,128)(2,1)}, bf16[128,4096]{1,0:T(8,128)(2,1)}) custom-call(s32[4]{0:T(128)} %pad_add_fusion.refs_0_, bf16[256,4096]{1,0:T(8,128)(2,1)} %get-tuple-element.46.signal_ref.refs_1_, bf16[256,4096]{1,0:T(8,128)(2,1)} %bitcast.37, ...), custom_call_target="tpu_custom_call" | custom-call | flops 4294967296 | bytes 25165824 | tf_op jit(solution)/shard_map/project/pallas_call | solution.py:369
  193.0 1.8 all-to-all-done.1
  194.8 1.3 collective-permute-start.26
  196.3 1.3 collective-permute-start.25
  197.6 1.2 collective-permute-start.27
  199.4 2.6 %collective-permute-start.29 = (bf16[16,128]{1,0:T(8,128)(2,1)S(1)}, bf16[16,128]{1,0:T(8,128)(2,1)S(1)}, u32[]{:S(2)}, u32[]{:S(2)}) collective-permute-start(bf16[16,128]{1,0:T(8,128)(2,1)S(1)} %get-tuple-element.72), channel_id=1, source_target_pairs={{0,96},{32,64},{64,32},{96,0},{1,97},{33,65},{65,33},{97,1},{2,98}... | collective-permute-start | bytes 12296 | tf_op jit(solution)/shard_map/ppermute | solution.py:434
  202.7 9.2 %all-to-all-start.2 = ((bf16[32,16,128]{2,1,0:T(8,128)(2,1)}), bf16[32,16,128]{2,1,0:T(8,128)(2,1)S(1)}, u32[]{:S(2)}, u32[]{:S(2)}) async-start(bf16[32,16,128]{2,1,0:T(8,128)(2,1)} %broadcast_in_dim.108), calls=%async_computation.2 | async-start | bytes 262144 | tf_op jit(solution)/shard_map/all_to_all | solution.py:435
  212.7 6.7 %backward_conv.2 = (bf16[256,4096]{1,0:T(8,128)(2,1)}, bf16[256,4096]{1,0:T(8,128)(2,1)}) custom-call(f32[256,256]{1,0:T(8,128)} %pad.9.base_ref, f32[1,4096]{1,0:T(1,128)} %bitcast.43, bf16[128,2048]{1,0:T(8,128)(2,1)} %get-tuple-element.63.head_ref, bf16[128,4096]{1,0:T(8,128)(2,1)} %get-tuple-element.62.tail_ref, bf16[128,2048]{1,0:T(8,128)(2,1)} %copy-done.14, ...), custom_call_target="tpu_custom_call" | custom-call | flops 2147483648 | bytes 6291456 | tf_op jit(solution)/shard_map/backward_conv/pallas_call | solution.py:192
  219.4 1.1 collective-permute-done.25.halo_ref
  221.3 6.7 %backward_conv.3 = (bf16[256,4096]{1,0:T(8,128)(2,1)}, bf16[256,4096]{1,0:T(8,128)(2,1)}) custom-call(f32[256,256]{1,0:T(8,128)} %pad.9.base_ref, f32[1,4096]{1,0:T(1,128)} %bitcast.44, bf16[128,2048]{1,0:T(8,128)(2,1)} %get-tuple-element.61.head_ref, bf16[128,4096]{1,0:T(8,128)(2,1)} %get-tuple-element.62.tail_ref, ...), custom_call_target="tpu_custom_call", output_to_operand_aliasing={{0}: (7, {}), {1}: (8, {})} | custom-call | flops 2147483648 | bytes 6291456 | tf_op jit(solution)/shard_map/backward_conv/pallas_call | solution.py:192
  (87 shorter events, 12.6 us)
Async XLA Ops:
  0.6 3.8 %copy-start = (bf16[128,64]{0,1:T(8,128)(2,1)S(1)}, bf16[128,64]{0,1:T(8,128)(2,1)}, u32[]{:S(2)}) copy-start(bf16[128,64]{0,1:T(8,128)(2,1)} %param.20) | copy-start | bytes 49156
  0.6 3.6 %copy-start.6 = (s32[128,16]{0,1:T(8,128)S(1)}, s32[128,16]{0,1:T(8,128)}, u32[]{:S(2)}) copy-start(s32[128,16]{0,1:T(8,128)} %param.16) | copy-start | bytes 24580
  0.7 3.6 %copy-start.7 = (f32[128]{0:T(128)S(1)}, f32[128]{0:T(128)}, u32[]{:S(2)}) copy-start(f32[128]{0:T(128)} %param.17) | copy-start | bytes 1540
  0.7 3.8 %copy-start.8 = (bf16[64,1024]{1,0:T(8,128)(2,1)S(1)}, bf16[64,1024]{1,0:T(8,128)(2,1)}, u32[]{:S(2)}) copy-start(bf16[64,1024]{1,0:T(8,128)(2,1)} %param.21) | copy-start | bytes 393220
  2.5 25.3 %collective-permute-start.8 = (bf16[128,4096]{1,0:T(8,128)(2,1)S(1)}, bf16[128,4096]{1,0:T(8,128)(2,1)}, u32[]{:S(2)}, u32[]{:S(2)}) collective-permute-start(bf16[128,4096]{1,0:T(8,128)(2,1)S(1)} %fusion.2), channel_id=1, source_target_pairs={{7,15},{15,23},{23,31},{39,47},{47,55},{55,63},{71,79},{79,87},{87... | collective-permute-start | bytes 3145736 | tf_op jit(solution)/shard_map/ppermute | solution.py:89
  7.0 8.6 %collective-permute-start = (bf16[128,1024]{1,0:T(8,128)(2,1)S(1)}, bf16[128,1024]{1,0:T(8,128)(2,1)S(1)}, u32[]{:S(2)}, u32[]{:S(2)}) collective-permute-start(bf16[128,1024]{1,0:T(8,128)(2,1)S(1)} %get-tuple-element.92), channel_id=1, source_target_pairs={{0,1},{32,34},{2,3},{34,36},{4,5},{36,38},{6,7},{38,32},{8,9},{40,... | collective-permute-start | bytes 786440 | tf_op jit(solution)/shard_map/ppermute | solution.py:54
  9.4 6.2 %collective-permute-start.1 = (bf16[128,1024]{1,0:T(8,128)(2,1)S(1)}, bf16[128,1024]{1,0:T(8,128)(2,1)S(1)}, u32[]{:S(2)}, u32[]{:S(2)}) collective-permute-start(bf16[128,1024]{1,0:T(8,128)(2,1)S(1)} %get-tuple-element.92), channel_id=1, source_target_pairs={{0,65},{32,38},{2,67},{34,32},{4,69},{36,34},{6,71},{38,36},{8,73}... | collective-permute-start | bytes 786440 | tf_op jit(solution)/shard_map/ppermute | solution.py:54
  15.6 5.4 %collective-permute-start.2 = (bf16[64,1024]{1,0:T(8,128)(2,1)S(1)}, bf16[64,1024]{1,0:T(8,128)(2,1)S(1)}, u32[]{:S(2)}, u32[]{:S(2)}) collective-permute-start(bf16[64,1024]{1,0:T(8,128)(2,1)S(1)} %slice.42), channel_id=1, source_target_pairs={{0,1},{32,34},{2,3},{34,36},{4,5},{36,38},{6,7},{38,32},{8,9},{40,... | collective-permute-start | bytes 393224 | tf_op jit(solution)/shard_map/ppermute | solution.py:54
  15.7 6.0 %collective-permute-start.3 = (bf16[64,1024]{1,0:T(8,128)(2,1)S(1)}, bf16[64,1024]{1,0:T(8,128)(2,1)S(1)}, u32[]{:S(2)}, u32[]{:S(2)}) collective-permute-start(bf16[64,1024]{1,0:T(8,128)(2,1)S(1)} %slice.43), channel_id=1, source_target_pairs={{0,65},{32,38},{2,67},{34,32},{4,69},{36,34},{6,71},{38,36},{8,73}... | collective-permute-start | bytes 393224 | tf_op jit(solution)/shard_map/ppermute | solution.py:54
  22.3 1.0 copy-start.13
  23.3 24.6 %collective-permute-start.5 = (bf16[512,1024]{1,0:T(8,128)(2,1)}, bf16[512,1024]{1,0:T(8,128)(2,1)S(1)}, u32[]{:S(2)}, u32[]{:S(2)}) collective-permute-start(bf16[512,1024]{1,0:T(8,128)(2,1)} %copy-done.13), channel_id=1, source_target_pairs={{0,8},{32,33},{2,10},{34,35},{4,12},{36,37},{6,14},{38,39},{8,16},... | collective-permute-start | bytes 3145736 | tf_op jit(solution)/shard_map/ppermute | solution.py:54
  26.5 23.6 %collective-permute-start.4 = (bf16[512,1024]{1,0:T(8,128)(2,1)}, bf16[512,1024]{1,0:T(8,128)(2,1)S(1)}, u32[]{:S(2)}, u32[]{:S(2)}) collective-permute-start(bf16[512,1024]{1,0:T(8,128)(2,1)} %copy-done.13), channel_id=1, source_target_pairs={{0,24},{32,97},{2,26},{34,99},{4,28},{36,101},{6,30},{38,103},{8,0... | collective-permute-start | bytes 3145736 | tf_op jit(solution)/shard_map/ppermute | solution.py:54
  28.9 41.4 %collective-permute-start.9 = (bf16[128,4096]{1,0:T(8,128)(2,1)}, bf16[128,4096]{1,0:T(8,128)(2,1)}, u32[]{:S(2)}, u32[]{:S(2)}) collective-permute-start(bf16[128,4096]{1,0:T(8,128)(2,1)} %broadcast_select_fusion.2), channel_id=1, source_target_pairs={{1,3},{3,5},{5,7},{9,11},{11,13},{13,15},{15,9},{17,19},{19,21},{2... | collective-permute-start | bytes 3145736 | tf_op jit(solution)/shard_map/ppermute | solution.py:94
  31.7 38.6 %all-to-all-start = ((bf16[128,32,128]{2,1,0:T(8,128)(2,1)}), bf16[128,32,128]{2,1,0:T(8,128)(2,1)}, u32[]{:S(2)}, u32[]{:S(2)}) async-start(bf16[128,32,128]{2,1,0:T(8,128)(2,1)} %broadcast_in_dim.102), calls=%async_computation | async-start | bytes 2097152 | tf_op jit(solution)/shard_map/all_to_all | solution.py:387
  48.8 18.8 %collective-permute-start.6 = (bf16[256,1024]{1,0:T(8,128)(2,1)}, bf16[256,1024]{1,0:T(8,128)(2,1)}, u32[]{:S(2)}, u32[]{:S(2)}) collective-permute-start(bf16[256,1024]{1,0:T(8,128)(2,1)} %slice.44), channel_id=1, source_target_pairs={{0,8},{32,33},{2,10},{34,35},{4,12},{36,37},{6,14},{38,39},{8,16},... | collective-permute-start | bytes 1572872 | tf_op jit(solution)/shard_map/ppermute | solution.py:54
  51.0 16.6 %collective-permute-start.7 = (bf16[256,1024]{1,0:T(8,128)(2,1)}, bf16[256,1024]{1,0:T(8,128)(2,1)}, u32[]{:S(2)}, u32[]{:S(2)}) collective-permute-start(bf16[256,1024]{1,0:T(8,128)(2,1)} %slice.45), channel_id=1, source_target_pairs={{0,24},{32,97},{2,26},{34,99},{4,28},{36,101},{6,30},{38,103},{8,0... | collective-permute-start | bytes 1572872 | tf_op jit(solution)/shard_map/ppermute | solution.py:54
  70.3 5.8 %copy-start.5 = (bf16[256,128]{1,0:T(8,128)(2,1)S(1)}, bf16[256,128]{1,0:T(8,128)(2,1)}, u32[]{:S(2)}) copy-start(bf16[256,128]{1,0:T(8,128)(2,1)} %param.18) | copy-start | bytes 196612
  70.3 10.6 %copy-start.3 = (bf16[1024,1024]{1,0:T(8,128)(2,1)S(1)}, bf16[1024,1024]{1,0:T(8,128)(2,1)}, u32[]{:S(2)}) copy-start(bf16[1024,1024]{1,0:T(8,128)(2,1)} %pad_maximum_fusion.refs_4_) | copy-start | bytes 6291460
  71.4 28.2 %collective-permute-start.10 = (bf16[128,4096]{1,0:T(8,128)(2,1)}, bf16[128,4096]{1,0:T(8,128)(2,1)S(1)}, u32[]{:S(2)}, u32[]{:S(2)}) collective-permute-start(bf16[128,4096]{1,0:T(8,128)(2,1)} %broadcast_select_fusion), channel_id=1, source_target_pairs={{0,1},{1,0},{2,3},{3,2},{4,5},{5,4},{6,7},{7,6},{8,9},{9,8},{10,11... | collective-permute-start | bytes 3145736 | tf_op jit(solution)/shard_map/ppermute | solution.py:99
  77.1 36.4 %collective-permute-start.11 = (bf16[1024,1024]{1,0:T(8,128)(2,1)}, bf16[1024,1024]{1,0:T(8,128)(2,1)}, u32[]{:S(2)}, u32[]{:S(2)}) collective-permute-start(bf16[1024,1024]{1,0:T(8,128)(2,1)} %constant_dynamic-update-slice_fusion.5.refs_3_), channel_id=1, source_target_pairs={{0,2},{32,40},{2,4},{34,42},{4,6},{36,44},{6,0},{38,46},{8,10},{40... | collective-permute-start | bytes 6291464 | tf_op jit(solution)/shard_map/ppermute | solution.py:54
  79.4 39.9 %collective-permute-start.17 = (bf16[1024,1024]{1,0:T(8,128)(2,1)}, bf16[1024,1024]{1,0:T(8,128)(2,1)S(1)}, u32[]{:S(2)}, u32[]{:S(2)}) collective-permute-start(bf16[1024,1024]{1,0:T(8,128)(2,1)} %constant_dynamic-update-slice_fusion.5.refs_3_), channel_id=1, source_target_pairs={{0,6},{32,56},{2,0},{34,58},{4,2},{36,60},{6,4},{38,62},{8,14},{40... | collective-permute-start | bytes 6291464 | tf_op jit(solution)/shard_map/ppermute | solution.py:54
  80.9 46.5 %collective-permute-start.18 = (bf16[1024,1024]{1,0:T(8,128)(2,1)S(1)}, bf16[1024,1024]{1,0:T(8,128)(2,1)}, u32[]{:S(2)}, u32[]{:S(2)}) collective-permute-start(bf16[1024,1024]{1,0:T(8,128)(2,1)S(1)} %copy-done.3), channel_id=1, source_target_pairs={{0,6},{32,56},{2,0},{34,58},{4,2},{36,60},{6,4},{38,62},{8,14},{40... | collective-permute-start | bytes 6291464 | tf_op jit(solution)/shard_map/ppermute | solution.py:54
  82.3 45.1 %collective-permute-start.14 = (bf16[1024,1024]{1,0:T(8,128)(2,1)S(1)}, bf16[1024,1024]{1,0:T(8,128)(2,1)}, u32[]{:S(2)}, u32[]{:S(2)}) collective-permute-start(bf16[1024,1024]{1,0:T(8,128)(2,1)S(1)} %copy-done.3), channel_id=1, source_target_pairs={{0,2},{32,40},{2,4},{34,42},{4,6},{36,44},{6,0},{38,46},{8,10},{40... | collective-permute-start | bytes 6291464 | tf_op jit(solution)/shard_map/ppermute | solution.py:54
  100.7 12.8 %copy-start.10 = (bf16[1024,1024]{1,0:T(8,128)(2,1)S(1)}, bf16[1024,1024]{1,0:T(8,128)(2,1)}, u32[]{:S(2)}) copy-start(bf16[1024,1024]{1,0:T(8,128)(2,1)} %constant_dynamic-update-slice_fusion.5.refs_3_) | copy-start | bytes 6291460
  112.7 15.2 %collective-permute-start.13 = (bf16[1024,1024]{1,0:T(8,128)(2,1)S(1)}, bf16[1024,1024]{1,0:T(8,128)(2,1)S(1)}, u32[]{:S(2)}, u32[]{:S(2)}) collective-permute-start(bf16[1024,1024]{1,0:T(8,128)(2,1)S(1)} %copy-done.3), channel_id=1, source_target_pairs={{0,32},{32,0},{2,34},{34,2},{4,36},{36,4},{6,38},{38,6},{8,40},{40... | collective-permute-start | bytes 6291464 | tf_op jit(solution)/shard_map/ppermute | solution.py:65
  113.5 14.5 %collective-permute-start.12 = (bf16[1024,1024]{1,0:T(8,128)(2,1)S(1)}, bf16[1024,1024]{1,0:T(8,128)(2,1)}, u32[]{:S(2)}, u32[]{:S(2)}) collective-permute-start(bf16[1024,1024]{1,0:T(8,128)(2,1)S(1)} %copy-done.10), channel_id=1, source_target_pairs={{0,32},{32,0},{2,34},{34,2},{4,36},{36,4},{6,38},{38,6},{8,40},{40... | collective-permute-start | bytes 6291464 | tf_op jit(solution)/shard_map/ppermute | solution.py:65
  119.3 8.7 %copy-start.9 = (bf16[1024,1024]{1,0:T(8,128)(2,1)}, bf16[1024,1024]{1,0:T(8,128)(2,1)S(1)}, u32[]{:S(2)}) copy-start(bf16[1024,1024]{1,0:T(8,128)(2,1)S(1)} %collective-permute-done.17.refs_11_) | copy-start | bytes 6291460
  119.3 12.3 %collective-permute-start.19 = (bf16[1024,1024]{1,0:T(8,128)(2,1)S(1)}, bf16[1024,1024]{1,0:T(8,128)(2,1)S(1)}, u32[]{:S(2)}, u32[]{:S(2)}) collective-permute-start(bf16[1024,1024]{1,0:T(8,128)(2,1)S(1)} %collective-permute-done.17.refs_11_), channel_id=1, source_target_pairs={{0,32},{32,0},{2,34},{34,2},{4,36},{36,4},{6,38},{38,6},{8,40},{40... | collective-permute-start | bytes 6291464 | tf_op jit(solution)/shard_map/ppermute | solution.py:65
  127.4 6.2 %collective-permute-start.15 = (bf16[1024,1024]{1,0:T(8,128)(2,1)}, bf16[1024,1024]{1,0:T(8,128)(2,1)}, u32[]{:S(2)}, u32[]{:S(2)}) collective-permute-start(bf16[1024,1024]{1,0:T(8,128)(2,1)} %collective-permute-done.11.refs_7_), channel_id=1, source_target_pairs={{0,32},{32,0},{2,34},{34,2},{4,36},{36,4},{6,38},{38,6},{8,40},{40... | collective-permute-start | bytes 6291464 | tf_op jit(solution)/shard_map/ppermute | solution.py:65
  127.4 7.5 %collective-permute-start.20 = (bf16[1024,1024]{1,0:T(8,128)(2,1)}, bf16[1024,1024]{1,0:T(8,128)(2,1)}, u32[]{:S(2)}, u32[]{:S(2)}) collective-permute-start(bf16[1024,1024]{1,0:T(8,128)(2,1)} %collective-permute-done.18.refs_12_), channel_id=1, source_target_pairs={{0,32},{32,0},{2,34},{34,2},{4,36},{36,4},{6,38},{38,6},{8,40},{40... | collective-permute-start | bytes 6291464 | tf_op jit(solution)/shard_map/ppermute | solution.py:65
  127.9 3.8 %copy-start.11 = (bf16[1024,1024]{1,0:T(8,128)(2,1)}, bf16[1024,1024]{1,0:T(8,128)(2,1)S(1)}, u32[]{:S(2)}) copy-start(bf16[1024,1024]{1,0:T(8,128)(2,1)S(1)} %collective-permute-done.13.refs_6_) | copy-start | bytes 6291460
  127.9 10.0 %collective-permute-start.16 = (bf16[1024,1024]{1,0:T(8,128)(2,1)}, bf16[1024,1024]{1,0:T(8,128)(2,1)}, u32[]{:S(2)}, u32[]{:S(2)}) collective-permute-start(bf16[1024,1024]{1,0:T(8,128)(2,1)} %collective-permute-done.14.refs_8_), channel_id=1, source_target_pairs={{0,32},{32,0},{2,34},{34,2},{4,36},{36,4},{6,38},{38,6},{8,40},{40... | collective-permute-start | bytes 6291464 | tf_op jit(solution)/shard_map/ppermute | solution.py:65
  128.0 36.5 %collective-permute-start.22 = (bf16[1024,1024]{1,0:T(8,128)(2,1)}, bf16[1024,1024]{1,0:T(8,128)(2,1)S(1)}, u32[]{:S(2)}, u32[]{:S(2)}) collective-permute-start(bf16[1024,1024]{1,0:T(8,128)(2,1)} %collective-permute-done.18.refs_12_), channel_id=1, source_target_pairs={{0,6},{32,56},{2,0},{34,58},{4,2},{36,60},{6,4},{38,62},{8,14},{40... | collective-permute-start | bytes 6291464 | tf_op jit(solution)/shard_map/ppermute | solution.py:54
  131.7 1.3 copy-start.12
  133.0 31.8 %collective-permute-start.21 = (bf16[1024,1024]{1,0:T(8,128)(2,1)}, bf16[1024,1024]{1,0:T(8,128)(2,1)}, u32[]{:S(2)}, u32[]{:S(2)}) collective-permute-start(bf16[1024,1024]{1,0:T(8,128)(2,1)} %collective-permute-done.11.refs_7_), channel_id=1, source_target_pairs={{0,2},{32,40},{2,4},{34,42},{4,6},{36,44},{6,0},{38,46},{8,10},{40... | collective-permute-start | bytes 6291464 | tf_op jit(solution)/shard_map/ppermute | solution.py:54
  164.5 11.7 %copy-start.2 = (bf16[1024,1024]{1,0:T(8,128)(2,1)}, bf16[1024,1024]{1,0:T(8,128)(2,1)S(1)}, u32[]{:S(2)}) copy-start(bf16[1024,1024]{1,0:T(8,128)(2,1)S(1)} %collective-permute-done.22.refs_6_) | copy-start | bytes 6291460
  164.5 11.7 %collective-permute-start.24 = (bf16[1024,1024]{1,0:T(8,128)(2,1)S(1)}, bf16[1024,1024]{1,0:T(8,128)(2,1)}, u32[]{:S(2)}, u32[]{:S(2)}) collective-permute-start(bf16[1024,1024]{1,0:T(8,128)(2,1)S(1)} %collective-permute-done.22.refs_6_), channel_id=1, source_target_pairs={{0,32},{32,0},{2,34},{34,2},{4,36},{36,4},{6,38},{38,6},{8,40},{40... | collective-permute-start | bytes 6291464 | tf_op jit(solution)/shard_map/ppermute | solution.py:65
  164.7 11.4 %collective-permute-start.23 = (bf16[1024,1024]{1,0:T(8,128)(2,1)}, bf16[1024,1024]{1,0:T(8,128)(2,1)}, u32[]{:S(2)}, u32[]{:S(2)}) collective-permute-start(bf16[1024,1024]{1,0:T(8,128)(2,1)} %collective-permute-done.21.refs_5_), channel_id=1, source_target_pairs={{0,32},{32,0},{2,34},{34,2},{4,36},{36,4},{6,38},{38,6},{8,40},{40... | collective-permute-start | bytes 6291464 | tf_op jit(solution)/shard_map/ppermute | solution.py:65
  165.1 29.7 %all-to-all-start.1 = ((bf16[128,32,128]{2,1,0:T(8,128)(2,1)}), bf16[128,32,128]{2,1,0:T(8,128)(2,1)S(1)}, u32[]{:S(2)}, u32[]{:S(2)}) async-start(bf16[128,32,128]{2,1,0:T(8,128)(2,1)} %adapter_terms.1), calls=%async_computation.1 | async-start | bytes 2097152 | tf_op jit(solution)/shard_map/all_to_all | solution.py:494
  194.8 17.0 %collective-permute-start.26 = (bf16[128,2048]{1,0:T(8,128)(2,1)}, bf16[128,2048]{1,0:T(8,128)(2,1)S(1)}, u32[]{:S(2)}, u32[]{:S(2)}) collective-permute-start(bf16[128,2048]{1,0:T(8,128)(2,1)} %get-tuple-element.63.head_ref), channel_id=1, source_target_pairs={{1,0},{2,1},{3,2},{4,3},{5,4},{6,5},{7,6},{8,7},{9,8},{10,9},{11,1... | collective-permute-start | bytes 1572872 | tf_op jit(solution)/shard_map/ppermute | solution.py:83
  196.3 24.2 %collective-permute-start.25 = (bf16[128,2048]{1,0:T(8,128)(2,1)}, bf16[128,2048]{1,0:T(8,128)(2,1)S(1)}, u32[]{:S(2)}, u32[]{:S(2)}) collective-permute-start(bf16[128,2048]{1,0:T(8,128)(2,1)} %get-tuple-element.61.head_ref), channel_id=1, source_target_pairs={{1,0},{2,1},{3,2},{4,3},{5,4},{6,5},{7,6},{8,7},{9,8},{10,9},{11,1... | collective-permute-start | bytes 1572872 | tf_op jit(solution)/shard_map/ppermute | solution.py:83
  197.6 30.4 %collective-permute-start.27 = (bf16[16,128]{1,0:T(8,128)(2,1)S(1)}, bf16[16,128]{1,0:T(8,128)(2,1)S(1)}, u32[]{:S(2)}, u32[]{:S(2)}) collective-permute-start(bf16[16,128]{1,0:T(8,128)(2,1)S(1)} %get-tuple-element.72), channel_id=1, source_target_pairs={{0,32},{32,0},{64,96},{96,64},{1,33},{33,1},{65,97},{97,65},{2,34}... | collective-permute-start | bytes 12296 | tf_op jit(solution)/shard_map/ppermute | solution.py:434
  198.8 29.3 %collective-permute-start.28 = (bf16[16,128]{1,0:T(8,128)(2,1)S(1)}, bf16[16,128]{1,0:T(8,128)(2,1)S(1)}, u32[]{:S(2)}, u32[]{:S(2)}) collective-permute-start(bf16[16,128]{1,0:T(8,128)(2,1)S(1)} %get-tuple-element.72), channel_id=1, source_target_pairs={{0,64},{32,96},{64,0},{96,32},{1,65},{33,97},{65,1},{97,33},{2,66}... | collective-permute-start | bytes 12296 | tf_op jit(solution)/shard_map/ppermute | solution.py:434
  199.4 28.7 %collective-permute-start.29 = (bf16[16,128]{1,0:T(8,128)(2,1)S(1)}, bf16[16,128]{1,0:T(8,128)(2,1)S(1)}, u32[]{:S(2)}, u32[]{:S(2)}) collective-permute-start(bf16[16,128]{1,0:T(8,128)(2,1)S(1)} %get-tuple-element.72), channel_id=1, source_target_pairs={{0,96},{32,64},{64,32},{96,0},{1,97},{33,65},{65,33},{97,1},{2,98}... | collective-permute-start | bytes 12296 | tf_op jit(solution)/shard_map/ppermute | solution.py:434
  202.7 25.4 %all-to-all-start.2 = ((bf16[32,16,128]{2,1,0:T(8,128)(2,1)}), bf16[32,16,128]{2,1,0:T(8,128)(2,1)S(1)}, u32[]{:S(2)}, u32[]{:S(2)}) async-start(bf16[32,16,128]{2,1,0:T(8,128)(2,1)} %broadcast_in_dim.108), calls=%async_computation.2 | async-start | bytes 262144 | tf_op jit(solution)/shard_map/all_to_all | solution.py:435
  211.8 0.8 copy-start.14
  220.5 0.8 copy-start.4
  221.3 8.1 %copy-start.1 = (bf16[128,64]{0,1:T(8,128)(2,1)S(1)}, bf16[128,64]{0,1:T(8,128)(2,1)}, u32[]{:S(2)}) copy-start(bf16[128,64]{0,1:T(8,128)(2,1)} %param.20) | copy-start | bytes 49156
